TPU v7x, 512 devices: a whole 4x4x16 slice. The times are simulated.
512 devices in a mesh: gx: 32 (over y, x, core), gy: 16 (over z).
Axes of the slice: x: 4, y: 4, z: 16, core: 2. Of those that a mesh axis runs over, the one named last changes fastest.
Arguments:
- initial: float32 [512, 1024, 128], P('gx', 'gy'), may hold values from -6 to 6, as said below
- material: int32 [512, 1024, 128], P('gx', 'gy'), may hold values from 0 to 7
- goal_faces: int32 [512, 1024, 128], P('gx', 'gy'), may hold values 0 or 1
- conductivity: float32 [8], replicated, may hold values from 0.2 to 2
Outputs:
- indicators: float32 [512, 1024, 128], P('gx', 'gy')
- sensitivity: float32 [512, 1024, 128], P('gx', 'gy')
Inputs may be any that keep to these rules, and one draw needn't show every extreme that they name: `initial`: temperatures.
All inputs are finite; a program needn't handle non-finite values. No bound on the sum of `goal_faces` on one device may be relied on, other than what follows from the above.
Results may differ from a plain program's by a relative error of at most 0.00002.
Values sent between devices are 32-bit elements; how exact they have to be, the bound alone decides.
A program may use at most 64 MiB of HBM per device.

v0:
```python
import jax
import jax.numpy as jnp
from jax import lax
from jax.sharding import PartitionSpec as P

step_size = 0.075


def padded_2(block, sides, width):
    for axis, dim in sides:
        count = lax.axis_size(axis)
        forward = [(i, i + 1) for i in range(count - 1)]
        backward = [(target, source) for source, target in forward]
        low = lax.ppermute(
            lax.slice_in_dim(block, block.shape[dim] - width, None, axis=dim), axis, forward
        )
        high = lax.ppermute(lax.slice_in_dim(block, 0, width, axis=dim), axis, backward)
        block = jnp.concatenate([low, block, high], axis=dim)
    return block


def shifted(value, axis, steps):
    count = lax.axis_size(axis)
    first, last = (max(0, -steps), min(count, count - steps))
    return lax.ppermute(value, axis, [(source, source + steps) for source in range(first, last)])


def lookup(material, conductivity):
    result = jnp.zeros(material.shape, jnp.float32)
    for which in range(conductivity.shape[0]):
        result = jnp.where(material == which, conductivity[which], result)
    return result


def deepen(padded):
    return jnp.pad(padded, ((0, 0), (0, 0), (1, 1)))


def neighbours(padded):
    return [
        padded[2:, 1:-1, 1:-1],
        padded[:-2, 1:-1, 1:-1],
        padded[1:-1, 2:, 1:-1],
        padded[1:-1, :-2, 1:-1],
        padded[1:-1, 1:-1, 2:],
        padded[1:-1, 1:-1, :-2],
    ]


def face_values(padded):
    centre = padded[1:-1, 1:-1, 1:-1]
    return [0.5 * (centre + other) for other in neighbours(padded)]


def divergence(field, padded, weights):
    total = jnp.zeros_like(field)
    for weight, other in zip(weights, neighbours(padded)):
        total = total + weight * (other - field)
    return total


def patch_mean(padded):
    rows = padded[:-2] + padded[1:-1] + padded[2:]
    rows = rows[:, :-2] + rows[:, 1:-1] + rows[:, 2:]
    rows = rows[:, :, :-2] + rows[:, :, 1:-1] + rows[:, :, 2:]
    return rows / 27.0


def per_step_plan(initial, material, goal_faces, conductivity):
    steps_count = 3
    conduct = lookup(material, conductivity)
    conduct_rim = padded_2(conduct, (("gx", 0), ("gy", 1)), 1)
    weights = face_values(deepen(conduct_rim))

    def state_slope(field):
        rim = padded_2(field, (("gx", 0), ("gy", 1)), 1)
        return divergence(field, deepen(rim), weights)

    states = [initial]
    slopes = []
    for section in range(steps_count):
        slopes.append(state_slope(states[-1]))
        states.append(states[-1] + step_size * slopes[-1])
    slopes.append(state_slope(states[-1]))
    residuals = [
        (states[section + 1] - states[section]) / step_size - slopes[section + 1]
        for section in range(steps_count)
    ]
    flux = goal_faces.astype(jnp.float32) * weights[0]
    edge_flux = shifted(flux[-1:], "gx", 1)
    adjoint = flux - jnp.concatenate([edge_flux, flux[:-1]], axis=0)
    indicators = jnp.zeros_like(initial)
    for section in range(steps_count - 1, -1, -1):
        full_rim = deepen(padded_2(adjoint, (("gx", 0), ("gy", 1)), 1))
        indicators = indicators + residuals[section] * (patch_mean(full_rim) - adjoint)
        adjoint = adjoint + step_size * divergence(adjoint, full_rim, weights)
    return (indicators, adjoint)


def per_device(initial, material, goal_faces, conductivity):
    return per_step_plan(initial, material, goal_faces, conductivity)


def solution(mesh):
    placed = (P("gx", "gy", None), P("gx", "gy", None), P("gx", "gy", None), P())
    return jax.shard_map(
        per_device,
        mesh=mesh,
        in_specs=placed,
        out_specs=(P("gx", "gy", None), P("gx", "gy", None)),
        check_vma=False,
    )
```

profile of v0, /device:TPU:240, one launch (start us, length us, event | category | flops | bytes accessed | tf_op | source)
XLA Modules:
  0.0 149.9 jit_solution(2951416493608210454)
XLA Ops:
  1.5 4.0 %collective-permute-start.1 = (f32[1,64,128]{2,1,0:T(8,128)S(1)}, f32[1,64,128]{2,1,0:T(8,128)S(1)}, u32[]{:S(2)}, u32[]{:S(2)}) collective-permute-start(f32[1,64,128]{2,1,0:T(8,128)S(1)} %get-tuple-element.39), channel_id=1, source_target_pairs={{16,0},{32,16},{48,32},{64,48},{80,64},{96,80},{112,96},{128,112},... | collective-permute-start | bytes 98312 | tf_op jit(solution)/shard_map/ppermute | solution.py:17
  5.5 1.9 %collective-permute-start.3 = (f32[1,64,128]{2,1,0:T(8,128)S(1)}, f32[1,64,128]{2,1,0:T(8,128)S(1)}, u32[]{:S(2)}, u32[]{:S(2)}) collective-permute-start(f32[1,64,128]{2,1,0:T(8,128)S(1)} %get-tuple-element.40), channel_id=1, source_target_pairs={{0,16},{16,32},{32,48},{48,64},{64,80},{80,96},{96,112},{112,128},... | collective-permute-start | bytes 98312 | tf_op jit(solution)/shard_map/ppermute | solution.py:14
  9.1 6.5 %select_select_fusion = f32[16,64,128]{2,1,0:T(8,128)S(1)} fusion(s32[16,64,128]{2,1,0:T(8,128)} %param.5, f32[]{:T(128)} %bitcast.7, f32[]{:T(128)} %bitcast.6, f32[]{:T(128)} %bitcast.5, f32[]{:T(128)} %bitcast.4, f32[]{:T(128)} %bitcast.3, f32[]{:T(128)} %bitcast.2, f32[]{:T(128)} %bitcast.1, f32[]{:T(128)} %bitcast), kind=kLoop, calls=%fused_computation.266 | loop fusion | flops 2097152 | bytes 1048608 | tf_op jit(solution)/shard_map/jit(_where)/select_n | solution.py:31
  15.6 1.9 %collective-permute-start.2 = (f32[1,64,128]{2,1,0:T(8,128)S(1)}, f32[1,64,128]{2,1,0:T(8,128)S(1)}, u32[]{:S(2)}, u32[]{:S(2)}) collective-permute-start(f32[1,64,128]{2,1,0:T(8,128)S(1)} %get-tuple-element.37), channel_id=1, source_target_pairs={{0,16},{16,32},{32,48},{48,64},{64,80},{80,96},{96,112},{112,128},... | collective-permute-start | bytes 98312 | tf_op jit(solution)/shard_map/ppermute | solution.py:14
  17.5 5.8 %collective-permute-start = (f32[1,64,128]{2,1,0:T(8,128)S(1)}, f32[1,64,128]{2,1,0:T(8,128)S(1)}, u32[]{:S(2)}, u32[]{:S(2)}) collective-permute-start(f32[1,64,128]{2,1,0:T(8,128)S(1)} %get-tuple-element.38), channel_id=1, source_target_pairs={{16,0},{32,16},{48,32},{64,48},{80,64},{96,80},{112,96},{128,112},... | collective-permute-start | bytes 98312 | tf_op jit(solution)/shard_map/ppermute | solution.py:17
  23.4 5.0 %collective-permute-start.7 = (f32[18,1,128]{2,1,0:T(1,128)S(1)}, f32[18,1,128]{2,1,0:T(1,128)S(1)}, u32[]{:S(2)}, u32[]{:S(2)}) collective-permute-start(f32[18,1,128]{2,1,0:T(1,128)S(1)} %get-tuple-element.23), channel_id=1, source_target_pairs={{0,1},{1,2},{2,3},{3,4},{4,5},{5,6},{6,7},{7,8},{8,9},{9,10},{10,1... | collective-permute-start | bytes 27656 | tf_op jit(solution)/shard_map/ppermute | solution.py:14
  28.4 1.9 %collective-permute-start.5 = (f32[18,1,128]{2,1,0:T(1,128)S(1)}, f32[18,1,128]{2,1,0:T(1,128)S(1)}, u32[]{:S(2)}, u32[]{:S(2)}) collective-permute-start(f32[18,1,128]{2,1,0:T(1,128)S(1)} %get-tuple-element.24), channel_id=1, source_target_pairs={{1,0},{2,1},{3,2},{4,3},{5,4},{6,5},{7,6},{8,7},{9,8},{10,9},{11,1... | collective-permute-start | bytes 27656 | tf_op jit(solution)/shard_map/ppermute | solution.py:17
  30.5 5.1 %collective-permute-start.6 = (f32[18,1,128]{2,1,0:T(1,128)S(1)}, f32[18,1,128]{2,1,0:T(1,128)S(1)}, u32[]{:S(2)}, u32[]{:S(2)}) collective-permute-start(f32[18,1,128]{2,1,0:T(1,128)S(1)} %get-tuple-element.21), channel_id=1, source_target_pairs={{0,1},{1,2},{2,3},{3,4},{4,5},{5,6},{6,7},{7,8},{8,9},{9,10},{10,1... | collective-permute-start | bytes 27656 | tf_op jit(solution)/shard_map/ppermute | solution.py:14
  35.7 1.9 %collective-permute-start.4 = (f32[18,1,128]{2,1,0:T(1,128)S(1)}, f32[18,1,128]{2,1,0:T(1,128)S(1)}, u32[]{:S(2)}, u32[]{:S(2)}) collective-permute-start(f32[18,1,128]{2,1,0:T(1,128)S(1)} %get-tuple-element.22), channel_id=1, source_target_pairs={{1,0},{2,1},{3,2},{4,3},{5,4},{6,5},{7,6},{8,7},{9,8},{10,9},{11,1... | collective-permute-start | bytes 27656 | tf_op jit(solution)/shard_map/ppermute | solution.py:17
  37.6 1.9 %collective-permute-start.20 = (f32[1,64,128]{2,1,0:T(8,128)S(1)}, f32[1,64,128]{2,1,0:T(8,128)S(1)}, u32[]{:S(2)}, u32[]{:S(2)}) collective-permute-start(f32[1,64,128]{2,1,0:T(8,128)S(1)} %slice.571), channel_id=1, source_target_pairs={{0,16},{16,32},{32,48},{48,64},{64,80},{80,96},{96,112},{112,128},... | collective-permute-start | bytes 98312 | tf_op jit(solution)/shard_map/ppermute | solution.py:25
  40.1 2.4 %collective-permute-done.4 = f32[18,1,128]{2,1,0:T(1,128)S(1)} collective-permute-done((f32[18,1,128]{2,1,0:T(1,128)S(1)}, f32[18,1,128]{2,1,0:T(1,128)S(1)}, u32[]{:S(2)}, u32[]{:S(2)}) %collective-permute-start.4) | collective-permute-done | bytes 9248 | tf_op jit(solution)/shard_map/ppermute | solution.py:17
  43.9 1.9 %collective-permute-start.9 = (f32[1,64,128]{2,1,0:T(8,128)S(1)}, f32[1,64,128]{2,1,0:T(8,128)S(1)}, u32[]{:S(2)}, u32[]{:S(2)}) collective-permute-start(f32[1,64,128]{2,1,0:T(8,128)S(1)} %get-tuple-element.29), channel_id=1, source_target_pairs={{0,16},{16,32},{32,48},{48,64},{64,80},{80,96},{96,112},{112,128},... | collective-permute-start | bytes 98312 | tf_op jit(solution)/shard_map/ppermute | solution.py:14
  45.8 5.8 %collective-permute-start.8 = (f32[1,64,128]{2,1,0:T(8,128)S(1)}, f32[1,64,128]{2,1,0:T(8,128)S(1)}, u32[]{:S(2)}, u32[]{:S(2)}) collective-permute-start(f32[1,64,128]{2,1,0:T(8,128)S(1)} %get-tuple-element.30), channel_id=1, source_target_pairs={{16,0},{32,16},{48,32},{64,48},{80,64},{96,80},{112,96},{128,112},... | collective-permute-start | bytes 98312 | tf_op jit(solution)/shard_map/ppermute | solution.py:17
  53.2 2.8 %collective-permute-start.11 = (f32[18,1,128]{2,1,0:T(1,128)S(1)}, f32[18,1,128]{2,1,0:T(1,128)S(1)}, u32[]{:S(2)}, u32[]{:S(2)}) collective-permute-start(f32[18,1,128]{2,1,0:T(1,128)S(1)} %get-tuple-element.13), channel_id=1, source_target_pairs={{0,1},{1,2},{2,3},{3,4},{4,5},{5,6},{6,7},{7,8},{8,9},{9,10},{10,1... | collective-permute-start | bytes 27656 | tf_op jit(solution)/shard_map/ppermute | solution.py:14
  55.9 3.1 %collective-permute-start.10 = (f32[18,1,128]{2,1,0:T(1,128)S(1)}, f32[18,1,128]{2,1,0:T(1,128)S(1)}, u32[]{:S(2)}, u32[]{:S(2)}) collective-permute-start(f32[18,1,128]{2,1,0:T(1,128)S(1)} %get-tuple-element.14), channel_id=1, source_target_pairs={{1,0},{2,1},{3,2},{4,3},{5,4},{6,5},{7,6},{8,7},{9,8},{10,9},{11,1... | collective-permute-start | bytes 27656 | tf_op jit(solution)/shard_map/ppermute | solution.py:17
  59.0 1.9 %collective-permute-start.21 = (f32[1,64,128]{2,1,0:T(8,128)S(1)}, f32[1,64,128]{2,1,0:T(8,128)S(1)}, u32[]{:S(2)}, u32[]{:S(2)}) collective-permute-start(f32[1,64,128]{2,1,0:T(8,128)S(1)} %get-tuple-element.35), channel_id=1, source_target_pairs={{0,16},{16,32},{32,48},{48,64},{64,80},{80,96},{96,112},{112,128},... | collective-permute-start | bytes 98312 | tf_op jit(solution)/shard_map/ppermute | solution.py:14
  61.0 5.8 %collective-permute-start.22 = (f32[1,64,128]{2,1,0:T(8,128)S(1)}, f32[1,64,128]{2,1,0:T(8,128)S(1)}, u32[]{:S(2)}, u32[]{:S(2)}) collective-permute-start(f32[1,64,128]{2,1,0:T(8,128)S(1)} %get-tuple-element.36), channel_id=1, source_target_pairs={{16,0},{32,16},{48,32},{64,48},{80,64},{96,80},{112,96},{128,112},... | collective-permute-start | bytes 98312 | tf_op jit(solution)/shard_map/ppermute | solution.py:17
  68.3 4.0 %collective-permute-start.23 = (f32[18,1,128]{2,1,0:T(1,128)S(1)}, f32[18,1,128]{2,1,0:T(1,128)S(1)}, u32[]{:S(2)}, u32[]{:S(2)}) collective-permute-start(f32[18,1,128]{2,1,0:T(1,128)S(1)} %get-tuple-element.19), channel_id=1, source_target_pairs={{0,1},{1,2},{2,3},{3,4},{4,5},{5,6},{6,7},{7,8},{8,9},{9,10},{10,1... | collective-permute-start | bytes 27656 | tf_op jit(solution)/shard_map/ppermute | solution.py:14
  76.2 5.8 %collective-permute-start.12 = (f32[1,64,128]{2,1,0:T(8,128)S(1)}, f32[1,64,128]{2,1,0:T(8,128)S(1)}, u32[]{:S(2)}, u32[]{:S(2)}) collective-permute-start(f32[1,64,128]{2,1,0:T(8,128)S(1)} %get-tuple-element.28), channel_id=1, source_target_pairs={{16,0},{32,16},{48,32},{64,48},{80,64},{96,80},{112,96},{128,112},... | collective-permute-start | bytes 98312 | tf_op jit(solution)/shard_map/ppermute | solution.py:17
  83.6 5.1 %collective-permute-start.15 = (f32[18,1,128]{2,1,0:T(1,128)S(1)}, f32[18,1,128]{2,1,0:T(1,128)S(1)}, u32[]{:S(2)}, u32[]{:S(2)}) collective-permute-start(f32[18,1,128]{2,1,0:T(1,128)S(1)} %get-tuple-element.11), channel_id=1, source_target_pairs={{0,1},{1,2},{2,3},{3,4},{4,5},{5,6},{6,7},{7,8},{8,9},{9,10},{10,1... | collective-permute-start | bytes 27656 | tf_op jit(solution)/shard_map/ppermute | solution.py:14
  88.8 1.9 %collective-permute-start.14 = (f32[18,1,128]{2,1,0:T(1,128)S(1)}, f32[18,1,128]{2,1,0:T(1,128)S(1)}, u32[]{:S(2)}, u32[]{:S(2)}) collective-permute-start(f32[18,1,128]{2,1,0:T(1,128)S(1)} %get-tuple-element.12), channel_id=1, source_target_pairs={{1,0},{2,1},{3,2},{4,3},{5,4},{6,5},{7,6},{8,7},{9,8},{10,9},{11,1... | collective-permute-start | bytes 27656 | tf_op jit(solution)/shard_map/ppermute | solution.py:17
  90.7 1.9 %collective-permute-start.25 = (f32[1,64,128]{2,1,0:T(8,128)S(1)}, f32[1,64,128]{2,1,0:T(8,128)S(1)}, u32[]{:S(2)}, u32[]{:S(2)}) collective-permute-start(f32[1,64,128]{2,1,0:T(8,128)S(1)} %get-tuple-element.33), channel_id=1, source_target_pairs={{0,16},{16,32},{32,48},{48,64},{64,80},{80,96},{96,112},{112,128},... | collective-permute-start | bytes 98312 | tf_op jit(solution)/shard_map/ppermute | solution.py:14
  92.6 5.8 %collective-permute-start.26 = (f32[1,64,128]{2,1,0:T(8,128)S(1)}, f32[1,64,128]{2,1,0:T(8,128)S(1)}, u32[]{:S(2)}, u32[]{:S(2)}) collective-permute-start(f32[1,64,128]{2,1,0:T(8,128)S(1)} %get-tuple-element.34), channel_id=1, source_target_pairs={{16,0},{32,16},{48,32},{64,48},{80,64},{96,80},{112,96},{128,112},... | collective-permute-start | bytes 98312 | tf_op jit(solution)/shard_map/ppermute | solution.py:17
  100.0 5.1 %collective-permute-start.27 = (f32[18,1,128]{2,1,0:T(1,128)S(1)}, f32[18,1,128]{2,1,0:T(1,128)S(1)}, u32[]{:S(2)}, u32[]{:S(2)}) collective-permute-start(f32[18,1,128]{2,1,0:T(1,128)S(1)} %get-tuple-element.17), channel_id=1, source_target_pairs={{0,1},{1,2},{2,3},{3,4},{4,5},{5,6},{6,7},{7,8},{8,9},{9,10},{10,1... | collective-permute-start | bytes 27656 | tf_op jit(solution)/shard_map/ppermute | solution.py:14
  109.0 5.8 %collective-permute-start.16 = (f32[1,64,128]{2,1,0:T(8,128)S(1)}, f32[1,64,128]{2,1,0:T(8,128)S(1)}, u32[]{:S(2)}, u32[]{:S(2)}) collective-permute-start(f32[1,64,128]{2,1,0:T(8,128)S(1)} %get-tuple-element.26), channel_id=1, source_target_pairs={{16,0},{32,16},{48,32},{64,48},{80,64},{96,80},{112,96},{128,112},... | collective-permute-start | bytes 98312 | tf_op jit(solution)/shard_map/ppermute | solution.py:17
  116.1 1.9 %collective-permute-start.29 = (f32[1,64,128]{2,1,0:T(8,128)S(1)}, f32[1,64,128]{2,1,0:T(8,128)S(1)}, u32[]{:S(2)}, u32[]{:S(2)}) collective-permute-start(f32[1,64,128]{2,1,0:T(8,128)S(1)} %get-tuple-element.31), channel_id=1, source_target_pairs={{0,16},{16,32},{32,48},{48,64},{64,80},{80,96},{96,112},{112,128},... | collective-permute-start | bytes 98312 | tf_op jit(solution)/shard_map/ppermute | solution.py:14
  118.1 5.8 %collective-permute-start.30 = (f32[1,64,128]{2,1,0:T(8,128)S(1)}, f32[1,64,128]{2,1,0:T(8,128)S(1)}, u32[]{:S(2)}, u32[]{:S(2)}) collective-permute-start(f32[1,64,128]{2,1,0:T(8,128)S(1)} %get-tuple-element.32), channel_id=1, source_target_pairs={{16,0},{32,16},{48,32},{64,48},{80,64},{96,80},{112,96},{128,112},... | collective-permute-start | bytes 98312 | tf_op jit(solution)/shard_map/ppermute | solution.py:17
  124.1 5.1 %collective-permute-start.19 = (f32[18,1,128]{2,1,0:T(1,128)S(1)}, f32[18,1,128]{2,1,0:T(1,128)S(1)}, u32[]{:S(2)}, u32[]{:S(2)}) collective-permute-start(f32[18,1,128]{2,1,0:T(1,128)S(1)} %get-tuple-element.9), channel_id=1, source_target_pairs={{0,1},{1,2},{2,3},{3,4},{4,5},{5,6},{6,7},{7,8},{8,9},{9,10},{10,1... | collective-permute-start | bytes 27656 | tf_op jit(solution)/shard_map/ppermute | solution.py:14
  131.2 5.1 %collective-permute-start.31 = (f32[18,1,128]{2,1,0:T(1,128)S(1)}, f32[18,1,128]{2,1,0:T(1,128)S(1)}, u32[]{:S(2)}, u32[]{:S(2)}) collective-permute-start(f32[18,1,128]{2,1,0:T(1,128)S(1)} %get-tuple-element.15), channel_id=1, source_target_pairs={{0,1},{1,2},{2,3},{3,4},{4,5},{5,6},{6,7},{7,8},{8,9},{9,10},{10,1... | collective-permute-start | bytes 27656 | tf_op jit(solution)/shard_map/ppermute | solution.py:14
  136.3 2.1 %collective-permute-start.32 = (f32[18,1,128]{2,1,0:T(1,128)S(1)}, f32[18,1,128]{2,1,0:T(1,128)S(1)}, u32[]{:S(2)}, u32[]{:S(2)}) collective-permute-start(f32[18,1,128]{2,1,0:T(1,128)S(1)} %get-tuple-element.16), channel_id=1, source_target_pairs={{1,0},{2,1},{3,2},{4,3},{5,4},{6,5},{7,6},{8,7},{9,8},{10,9},{11,1... | collective-permute-start | bytes 27656 | tf_op jit(solution)/shard_map/ppermute | solution.py:17
  139.0 4.1 %collective-permute-done.32 = f32[18,1,128]{2,1,0:T(1,128)S(1)} collective-permute-done((f32[18,1,128]{2,1,0:T(1,128)S(1)}, f32[18,1,128]{2,1,0:T(1,128)S(1)}, u32[]{:S(2)}, u32[]{:S(2)}) %collective-permute-start.32) | collective-permute-done | bytes 9248 | tf_op jit(solution)/shard_map/ppermute | solution.py:17
  145.5 4.3 %fusion.21 = f32[16,64,128]{2,1,0:T(8,128)} fusion(f32[16,64,130]{2,1,0:T(8,128)S(1)} %slice_add_fusion.6, f32[16,64,128]{2,1,0:T(8,128)S(1)} %fusion.46, f32[16,64,130]{2,1,0:T(8,128)S(1)} %slice_add_fusion.8, f32[16,64,130]{2,1,0:T(8,128)S(1)} %slice_add_fusion.10, f32[16,64,128]{2,1,0:T(8,128)S(1)} %get-tuple-element.8, ...), kind=kLoop, calls=%fused_computation.76 | loop fusion | flops 12845056 | bytes 13359104 | tf_op jit(solution)/shard_map/add | solution.py:95
  (84 shorter events, 25.0 us)
Async XLA Ops:
  1.5 21.8 %collective-permute-start.1 = (f32[1,64,128]{2,1,0:T(8,128)S(1)}, f32[1,64,128]{2,1,0:T(8,128)S(1)}, u32[]{:S(2)}, u32[]{:S(2)}) collective-permute-start(f32[1,64,128]{2,1,0:T(8,128)S(1)} %get-tuple-element.39), channel_id=1, source_target_pairs={{16,0},{32,16},{48,32},{64,48},{80,64},{96,80},{112,96},{128,112},... | collective-permute-start | bytes 98312 | tf_op jit(solution)/shard_map/ppermute | solution.py:17
  5.5 17.7 %collective-permute-start.3 = (f32[1,64,128]{2,1,0:T(8,128)S(1)}, f32[1,64,128]{2,1,0:T(8,128)S(1)}, u32[]{:S(2)}, u32[]{:S(2)}) collective-permute-start(f32[1,64,128]{2,1,0:T(8,128)S(1)} %get-tuple-element.40), channel_id=1, source_target_pairs={{0,16},{16,32},{32,48},{48,64},{64,80},{80,96},{96,112},{112,128},... | collective-permute-start | bytes 98312 | tf_op jit(solution)/shard_map/ppermute | solution.py:14
  15.6 14.9 %collective-permute-start.2 = (f32[1,64,128]{2,1,0:T(8,128)S(1)}, f32[1,64,128]{2,1,0:T(8,128)S(1)}, u32[]{:S(2)}, u32[]{:S(2)}) collective-permute-start(f32[1,64,128]{2,1,0:T(8,128)S(1)} %get-tuple-element.37), channel_id=1, source_target_pairs={{0,16},{16,32},{32,48},{48,64},{64,80},{80,96},{96,112},{112,128},... | collective-permute-start | bytes 98312 | tf_op jit(solution)/shard_map/ppermute | solution.py:14
  17.5 12.9 %collective-permute-start = (f32[1,64,128]{2,1,0:T(8,128)S(1)}, f32[1,64,128]{2,1,0:T(8,128)S(1)}, u32[]{:S(2)}, u32[]{:S(2)}) collective-permute-start(f32[1,64,128]{2,1,0:T(8,128)S(1)} %get-tuple-element.38), channel_id=1, source_target_pairs={{16,0},{32,16},{48,32},{64,48},{80,64},{96,80},{112,96},{128,112},... | collective-permute-start | bytes 98312 | tf_op jit(solution)/shard_map/ppermute | solution.py:17
  23.4 16.2 %collective-permute-start.7 = (f32[18,1,128]{2,1,0:T(1,128)S(1)}, f32[18,1,128]{2,1,0:T(1,128)S(1)}, u32[]{:S(2)}, u32[]{:S(2)}) collective-permute-start(f32[18,1,128]{2,1,0:T(1,128)S(1)} %get-tuple-element.23), channel_id=1, source_target_pairs={{0,1},{1,2},{2,3},{3,4},{4,5},{5,6},{6,7},{7,8},{8,9},{9,10},{10,1... | collective-permute-start | bytes 27656 | tf_op jit(solution)/shard_map/ppermute | solution.py:14
  28.4 11.1 %collective-permute-start.5 = (f32[18,1,128]{2,1,0:T(1,128)S(1)}, f32[18,1,128]{2,1,0:T(1,128)S(1)}, u32[]{:S(2)}, u32[]{:S(2)}) collective-permute-start(f32[18,1,128]{2,1,0:T(1,128)S(1)} %get-tuple-element.24), channel_id=1, source_target_pairs={{1,0},{2,1},{3,2},{4,3},{5,4},{6,5},{7,6},{8,7},{9,8},{10,9},{11,1... | collective-permute-start | bytes 27656 | tf_op jit(solution)/shard_map/ppermute | solution.py:17
  30.5 9.5 %collective-permute-start.6 = (f32[18,1,128]{2,1,0:T(1,128)S(1)}, f32[18,1,128]{2,1,0:T(1,128)S(1)}, u32[]{:S(2)}, u32[]{:S(2)}) collective-permute-start(f32[18,1,128]{2,1,0:T(1,128)S(1)} %get-tuple-element.21), channel_id=1, source_target_pairs={{0,1},{1,2},{2,3},{3,4},{4,5},{5,6},{6,7},{7,8},{8,9},{9,10},{10,1... | collective-permute-start | bytes 27656 | tf_op jit(solution)/shard_map/ppermute | solution.py:14
  35.7 6.8 %collective-permute-start.4 = (f32[18,1,128]{2,1,0:T(1,128)S(1)}, f32[18,1,128]{2,1,0:T(1,128)S(1)}, u32[]{:S(2)}, u32[]{:S(2)}) collective-permute-start(f32[18,1,128]{2,1,0:T(1,128)S(1)} %get-tuple-element.22), channel_id=1, source_target_pairs={{1,0},{2,1},{3,2},{4,3},{5,4},{6,5},{7,6},{8,7},{9,8},{10,9},{11,1... | collective-permute-start | bytes 27656 | tf_op jit(solution)/shard_map/ppermute | solution.py:17
  37.6 14.0 %collective-permute-start.20 = (f32[1,64,128]{2,1,0:T(8,128)S(1)}, f32[1,64,128]{2,1,0:T(8,128)S(1)}, u32[]{:S(2)}, u32[]{:S(2)}) collective-permute-start(f32[1,64,128]{2,1,0:T(8,128)S(1)} %slice.571), channel_id=1, source_target_pairs={{0,16},{16,32},{32,48},{48,64},{64,80},{80,96},{96,112},{112,128},... | collective-permute-start | bytes 98312 | tf_op jit(solution)/shard_map/ppermute | solution.py:25
  43.9 7.8 %collective-permute-start.9 = (f32[1,64,128]{2,1,0:T(8,128)S(1)}, f32[1,64,128]{2,1,0:T(8,128)S(1)}, u32[]{:S(2)}, u32[]{:S(2)}) collective-permute-start(f32[1,64,128]{2,1,0:T(8,128)S(1)} %get-tuple-element.29), channel_id=1, source_target_pairs={{0,16},{16,32},{32,48},{48,64},{64,80},{80,96},{96,112},{112,128},... | collective-permute-start | bytes 98312 | tf_op jit(solution)/shard_map/ppermute | solution.py:14
  45.8 7.3 %collective-permute-start.8 = (f32[1,64,128]{2,1,0:T(8,128)S(1)}, f32[1,64,128]{2,1,0:T(8,128)S(1)}, u32[]{:S(2)}, u32[]{:S(2)}) collective-permute-start(f32[1,64,128]{2,1,0:T(8,128)S(1)} %get-tuple-element.30), channel_id=1, source_target_pairs={{16,0},{32,16},{48,32},{64,48},{80,64},{96,80},{112,96},{128,112},... | collective-permute-start | bytes 98312 | tf_op jit(solution)/shard_map/ppermute | solution.py:17
  53.2 13.6 %collective-permute-start.11 = (f32[18,1,128]{2,1,0:T(1,128)S(1)}, f32[18,1,128]{2,1,0:T(1,128)S(1)}, u32[]{:S(2)}, u32[]{:S(2)}) collective-permute-start(f32[18,1,128]{2,1,0:T(1,128)S(1)} %get-tuple-element.13), channel_id=1, source_target_pairs={{0,1},{1,2},{2,3},{3,4},{4,5},{5,6},{6,7},{7,8},{8,9},{9,10},{10,1... | collective-permute-start | bytes 27656 | tf_op jit(solution)/shard_map/ppermute | solution.py:14
  55.9 10.8 %collective-permute-start.10 = (f32[18,1,128]{2,1,0:T(1,128)S(1)}, f32[18,1,128]{2,1,0:T(1,128)S(1)}, u32[]{:S(2)}, u32[]{:S(2)}) collective-permute-start(f32[18,1,128]{2,1,0:T(1,128)S(1)} %get-tuple-element.14), channel_id=1, source_target_pairs={{1,0},{2,1},{3,2},{4,3},{5,4},{6,5},{7,6},{8,7},{9,8},{10,9},{11,1... | collective-permute-start | bytes 27656 | tf_op jit(solution)/shard_map/ppermute | solution.py:17
  59.0 8.9 %collective-permute-start.21 = (f32[1,64,128]{2,1,0:T(8,128)S(1)}, f32[1,64,128]{2,1,0:T(8,128)S(1)}, u32[]{:S(2)}, u32[]{:S(2)}) collective-permute-start(f32[1,64,128]{2,1,0:T(8,128)S(1)} %get-tuple-element.35), channel_id=1, source_target_pairs={{0,16},{16,32},{32,48},{48,64},{64,80},{80,96},{96,112},{112,128},... | collective-permute-start | bytes 98312 | tf_op jit(solution)/shard_map/ppermute | solution.py:14
  61.0 7.3 %collective-permute-start.22 = (f32[1,64,128]{2,1,0:T(8,128)S(1)}, f32[1,64,128]{2,1,0:T(8,128)S(1)}, u32[]{:S(2)}, u32[]{:S(2)}) collective-permute-start(f32[1,64,128]{2,1,0:T(8,128)S(1)} %get-tuple-element.36), channel_id=1, source_target_pairs={{16,0},{32,16},{48,32},{64,48},{80,64},{96,80},{112,96},{128,112},... | collective-permute-start | bytes 98312 | tf_op jit(solution)/shard_map/ppermute | solution.py:17
  68.3 13.6 %collective-permute-start.23 = (f32[18,1,128]{2,1,0:T(1,128)S(1)}, f32[18,1,128]{2,1,0:T(1,128)S(1)}, u32[]{:S(2)}, u32[]{:S(2)}) collective-permute-start(f32[18,1,128]{2,1,0:T(1,128)S(1)} %get-tuple-element.19), channel_id=1, source_target_pairs={{0,1},{1,2},{2,3},{3,4},{4,5},{5,6},{6,7},{7,8},{8,9},{9,10},{10,1... | collective-permute-start | bytes 27656 | tf_op jit(solution)/shard_map/ppermute | solution.py:14
  72.3 9.6 %collective-permute-start.24 = (f32[18,1,128]{2,1,0:T(1,128)S(1)}, f32[18,1,128]{2,1,0:T(1,128)S(1)}, u32[]{:S(2)}, u32[]{:S(2)}) collective-permute-start(f32[18,1,128]{2,1,0:T(1,128)S(1)} %get-tuple-element.20), channel_id=1, source_target_pairs={{1,0},{2,1},{3,2},{4,3},{5,4},{6,5},{7,6},{8,7},{9,8},{10,9},{11,1... | collective-permute-start | bytes 27656 | tf_op jit(solution)/shard_map/ppermute | solution.py:17
  74.3 9.3 %collective-permute-start.13 = (f32[1,64,128]{2,1,0:T(8,128)S(1)}, f32[1,64,128]{2,1,0:T(8,128)S(1)}, u32[]{:S(2)}, u32[]{:S(2)}) collective-permute-start(f32[1,64,128]{2,1,0:T(8,128)S(1)} %get-tuple-element.27), channel_id=1, source_target_pairs={{0,16},{16,32},{32,48},{48,64},{64,80},{80,96},{96,112},{112,128},... | collective-permute-start | bytes 98312 | tf_op jit(solution)/shard_map/ppermute | solution.py:14
  76.2 7.4 %collective-permute-start.12 = (f32[1,64,128]{2,1,0:T(8,128)S(1)}, f32[1,64,128]{2,1,0:T(8,128)S(1)}, u32[]{:S(2)}, u32[]{:S(2)}) collective-permute-start(f32[1,64,128]{2,1,0:T(8,128)S(1)} %get-tuple-element.28), channel_id=1, source_target_pairs={{16,0},{32,16},{48,32},{64,48},{80,64},{96,80},{112,96},{128,112},... | collective-permute-start | bytes 98312 | tf_op jit(solution)/shard_map/ppermute | solution.py:17
  83.6 14.8 %collective-permute-start.15 = (f32[18,1,128]{2,1,0:T(1,128)S(1)}, f32[18,1,128]{2,1,0:T(1,128)S(1)}, u32[]{:S(2)}, u32[]{:S(2)}) collective-permute-start(f32[18,1,128]{2,1,0:T(1,128)S(1)} %get-tuple-element.11), channel_id=1, source_target_pairs={{0,1},{1,2},{2,3},{3,4},{4,5},{5,6},{6,7},{7,8},{8,9},{9,10},{10,1... | collective-permute-start | bytes 27656 | tf_op jit(solution)/shard_map/ppermute | solution.py:14
  88.8 9.6 %collective-permute-start.14 = (f32[18,1,128]{2,1,0:T(1,128)S(1)}, f32[18,1,128]{2,1,0:T(1,128)S(1)}, u32[]{:S(2)}, u32[]{:S(2)}) collective-permute-start(f32[18,1,128]{2,1,0:T(1,128)S(1)} %get-tuple-element.12), channel_id=1, source_target_pairs={{1,0},{2,1},{3,2},{4,3},{5,4},{6,5},{7,6},{8,7},{9,8},{10,9},{11,1... | collective-permute-start | bytes 27656 | tf_op jit(solution)/shard_map/ppermute | solution.py:17
  90.7 9.0 %collective-permute-start.25 = (f32[1,64,128]{2,1,0:T(8,128)S(1)}, f32[1,64,128]{2,1,0:T(8,128)S(1)}, u32[]{:S(2)}, u32[]{:S(2)}) collective-permute-start(f32[1,64,128]{2,1,0:T(8,128)S(1)} %get-tuple-element.33), channel_id=1, source_target_pairs={{0,16},{16,32},{32,48},{48,64},{64,80},{80,96},{96,112},{112,128},... | collective-permute-start | bytes 98312 | tf_op jit(solution)/shard_map/ppermute | solution.py:14
  92.6 7.3 %collective-permute-start.26 = (f32[1,64,128]{2,1,0:T(8,128)S(1)}, f32[1,64,128]{2,1,0:T(8,128)S(1)}, u32[]{:S(2)}, u32[]{:S(2)}) collective-permute-start(f32[1,64,128]{2,1,0:T(8,128)S(1)} %get-tuple-element.34), channel_id=1, source_target_pairs={{16,0},{32,16},{48,32},{64,48},{80,64},{96,80},{112,96},{128,112},... | collective-permute-start | bytes 98312 | tf_op jit(solution)/shard_map/ppermute | solution.py:17
  100.0 14.8 %collective-permute-start.27 = (f32[18,1,128]{2,1,0:T(1,128)S(1)}, f32[18,1,128]{2,1,0:T(1,128)S(1)}, u32[]{:S(2)}, u32[]{:S(2)}) collective-permute-start(f32[18,1,128]{2,1,0:T(1,128)S(1)} %get-tuple-element.17), channel_id=1, source_target_pairs={{0,1},{1,2},{2,3},{3,4},{4,5},{5,6},{6,7},{7,8},{8,9},{9,10},{10,1... | collective-permute-start | bytes 27656 | tf_op jit(solution)/shard_map/ppermute | solution.py:14
  105.1 9.6 %collective-permute-start.28 = (f32[18,1,128]{2,1,0:T(1,128)S(1)}, f32[18,1,128]{2,1,0:T(1,128)S(1)}, u32[]{:S(2)}, u32[]{:S(2)}) collective-permute-start(f32[18,1,128]{2,1,0:T(1,128)S(1)} %get-tuple-element.18), channel_id=1, source_target_pairs={{1,0},{2,1},{3,2},{4,3},{5,4},{6,5},{7,6},{8,7},{9,8},{10,9},{11,1... | collective-permute-start | bytes 27656 | tf_op jit(solution)/shard_map/ppermute | solution.py:17
  107.1 17.0 %collective-permute-start.17 = (f32[1,64,128]{2,1,0:T(8,128)S(1)}, f32[1,64,128]{2,1,0:T(8,128)S(1)}, u32[]{:S(2)}, u32[]{:S(2)}) collective-permute-start(f32[1,64,128]{2,1,0:T(8,128)S(1)} %get-tuple-element.25), channel_id=1, source_target_pairs={{0,16},{16,32},{32,48},{48,64},{64,80},{80,96},{96,112},{112,128},... | collective-permute-start | bytes 98312 | tf_op jit(solution)/shard_map/ppermute | solution.py:14
  109.0 15.0 %collective-permute-start.16 = (f32[1,64,128]{2,1,0:T(8,128)S(1)}, f32[1,64,128]{2,1,0:T(8,128)S(1)}, u32[]{:S(2)}, u32[]{:S(2)}) collective-permute-start(f32[1,64,128]{2,1,0:T(8,128)S(1)} %get-tuple-element.26), channel_id=1, source_target_pairs={{16,0},{32,16},{48,32},{64,48},{80,64},{96,80},{112,96},{128,112},... | collective-permute-start | bytes 98312 | tf_op jit(solution)/shard_map/ppermute | solution.py:17
  116.1 15.0 %collective-permute-start.29 = (f32[1,64,128]{2,1,0:T(8,128)S(1)}, f32[1,64,128]{2,1,0:T(8,128)S(1)}, u32[]{:S(2)}, u32[]{:S(2)}) collective-permute-start(f32[1,64,128]{2,1,0:T(8,128)S(1)} %get-tuple-element.31), channel_id=1, source_target_pairs={{0,16},{16,32},{32,48},{48,64},{64,80},{80,96},{96,112},{112,128},... | collective-permute-start | bytes 98312 | tf_op jit(solution)/shard_map/ppermute | solution.py:14
  118.1 13.1 %collective-permute-start.30 = (f32[1,64,128]{2,1,0:T(8,128)S(1)}, f32[1,64,128]{2,1,0:T(8,128)S(1)}, u32[]{:S(2)}, u32[]{:S(2)}) collective-permute-start(f32[1,64,128]{2,1,0:T(8,128)S(1)} %get-tuple-element.32), channel_id=1, source_target_pairs={{16,0},{32,16},{48,32},{64,48},{80,64},{96,80},{112,96},{128,112},... | collective-permute-start | bytes 98312 | tf_op jit(solution)/shard_map/ppermute | solution.py:17
  124.1 14.4 %collective-permute-start.19 = (f32[18,1,128]{2,1,0:T(1,128)S(1)}, f32[18,1,128]{2,1,0:T(1,128)S(1)}, u32[]{:S(2)}, u32[]{:S(2)}) collective-permute-start(f32[18,1,128]{2,1,0:T(1,128)S(1)} %get-tuple-element.9), channel_id=1, source_target_pairs={{0,1},{1,2},{2,3},{3,4},{4,5},{5,6},{6,7},{7,8},{8,9},{9,10},{10,1... | collective-permute-start | bytes 27656 | tf_op jit(solution)/shard_map/ppermute | solution.py:14
  129.2 9.2 %collective-permute-start.18 = (f32[18,1,128]{2,1,0:T(1,128)S(1)}, f32[18,1,128]{2,1,0:T(1,128)S(1)}, u32[]{:S(2)}, u32[]{:S(2)}) collective-permute-start(f32[18,1,128]{2,1,0:T(1,128)S(1)} %get-tuple-element.10), channel_id=1, source_target_pairs={{1,0},{2,1},{3,2},{4,3},{5,4},{6,5},{7,6},{8,7},{9,8},{10,9},{11,1... | collective-permute-start | bytes 27656 | tf_op jit(solution)/shard_map/ppermute | solution.py:17
  131.2 7.8 %collective-permute-start.31 = (f32[18,1,128]{2,1,0:T(1,128)S(1)}, f32[18,1,128]{2,1,0:T(1,128)S(1)}, u32[]{:S(2)}, u32[]{:S(2)}) collective-permute-start(f32[18,1,128]{2,1,0:T(1,128)S(1)} %get-tuple-element.15), channel_id=1, source_target_pairs={{0,1},{1,2},{2,3},{3,4},{4,5},{5,6},{6,7},{7,8},{8,9},{9,10},{10,1... | collective-permute-start | bytes 27656 | tf_op jit(solution)/shard_map/ppermute | solution.py:14
  (3 other events, 59.1 us)
where the time goes:
time: 151 us; the launch traced here: 150 us
  starting transfers between devices  116 us (77%)
  other arithmetic  21.5 us (14%)
  waiting for transfers between devices  8.65 us (6%)
  local copies, waits for them, and re-layouts  2.66 us (2%)
    ppermute x16, starting transfers between devices, padded_2(): lax.ppermute(lax.slice_in_dim(block, 0, width, axis=dim), axis, backward)  60.9 us
    ppermute x16, starting transfers between devices, padded_2(): lax.ppermute(lax.slice_in_dim(block, block.shape[dim] - width, None, axis...  52.8 us
    ppermute x16, waiting for transfers between devices, padded_2(): lax.ppermute(lax.slice_in_dim(block, 0, width, axis=dim), axis, backward)  8.6 us
    select_n x1, other arithmetic, lookup(): result = jnp.where(material == which, conductivity[which], result)  6.48 us
    add x1, other arithmetic, per_step_plan(): indicators + residuals[section] * (patch_mean(full_rim) - adjoint)  4.34 us
    concatenate x12, other arithmetic, padded_2(): block = jnp.concatenate([low, block, high], axis=dim)  4.01 us
    add x3, other arithmetic, per_step_plan(): adjoint = adjoint + step_size * divergence(adjoint, full_rim, weights)  3.12 us
  transfers between devices with their start and end apart: 33, of which 5 were waited for; matrix products, arithmetic and copies ran while one was open for 11% of the time, Pallas kernels for 0%

commit v1 on v0

v1 whole, which is shorter than its diff:
```python
import functools

import jax
import jax.numpy as jnp
from jax import lax
from jax.experimental import pallas as pl
from jax.experimental.pallas import tpu as pltpu
from jax.sharding import PartitionSpec as P

MESH = pl.DeviceIdType.MESH
step_size = 0.075
HALO = 4
R0 = 8


def kernel(
    nx, ny, cond_in,
    u_in, m_in, g_in, u_rows, m_rows, g_rows,
    ind_out, sens_out,
    u_own, m_own, g_own, xu, xm, xg, yu, ym, yg, cu, cm, cg,
    K, WX, WY, WZ, C, G, V0, V1, V2, V3, Z3, Z2, Z1, T,
    cond, load_sem, x_send, x_recv, y_send, y_recv, c_send, c_recv,
):
    depth, rows, lanes = u_in.shape
    planes = depth + 2 * HALO
    ext = rows + 2 * HALO
    own0 = R0 + HALO
    gx, gy = lax.axis_index("gx"), lax.axis_index("gy")
    has_left, has_right = gx > 0, gx < nx - 1
    has_down, has_up = gy > 0, gy < ny - 1
    left, right = (gx - 1, gy), (gx + 1, gy)
    down, up = (gx, gy - 1), (gx, gy + 1)

    loads = [
        pltpu.make_async_copy(src, dst, load_sem.at[i])
        for i, (src, dst) in enumerate(((u_in, u_own), (m_in, m_own), (g_in, g_own), (cond_in, cond)))
    ]
    for load in loads:
        load.start()

    barrier = pltpu.get_barrier_semaphore()
    sides = ((has_left, left), (has_right, right), (has_down, down), (has_up, up))
    for there, who in sides:
        @pl.when(there)
        def _():
            pl.semaphore_signal(barrier, inc=1, device_id=who, device_id_type=MESH)
    pl.semaphore_wait(barrier, sum(there.astype(jnp.int32) for there, _ in sides))

    ins = (u_in, m_in, g_in)
    in_rows = (u_rows, m_rows, g_rows)
    xs, ys, cs = (xu, xm, xg), (yu, ym, yg), (cu, cm, cg)

    def remote(src, dst, send, recv, who):
        return pltpu.make_async_remote_copy(
            src_ref=src, dst_ref=dst, send_sem=send, recv_sem=recv,
            device_id=who, device_id_type=MESH,
        )

    def y_copy(side, a):
        who = up if side == 0 else down
        group = in_rows[a].shape[1] - 1 if side == 0 else 0
        return remote(in_rows[a].at[:, group], ys[a].at[side],
                      y_send.at[side, a], y_recv.at[side, a], who)

    def x_copy(side, j, a):
        who = right if side == 0 else left
        plane = depth - HALO + j if side == 0 else j
        return remote(ins[a].at[plane], xs[a].at[side, j],
                      x_send.at[side, j, a], x_recv.at[side, j, a], who)

    def c_copy(side, y_side, a):
        who = right if side == 0 else left
        first = depth - HALO if side == 0 else 0
        return remote(ys[a].at[y_side, pl.ds(first, HALO)], cs[a].at[side, y_side],
                      c_send.at[side, y_side, a], c_recv.at[side, y_side, a], who)

    sends_to = ((has_right, has_left), (has_up, has_down))
    comes_from = ((has_left, has_right), (has_down, has_up))

    def x_parts(side):
        order = (3, 2, 1, 0) if side == 0 else (0, 1, 2, 3)
        return [(j, a) for j in order for a in range(3) if not (side == 1 and j == 3 and a == 2)]

    for side in range(2):
        @pl.when(sends_to[1][side])
        def _():
            for a in range(3):
                y_copy(side, a).start()
        @pl.when(sends_to[0][side])
        def _():
            for j, a in x_parts(side):
                x_copy(side, j, a).start()

    for load in loads:
        load.wait()

    scale = 0.5 * step_size
    table = [cond[i] * scale for i in range(cond.shape[0])]

    def lookup(m):
        k = jnp.full(m.shape, table[0], jnp.float32)
        for i in range(1, len(table)):
            k = jnp.where(m == i, table[i], k)
        return k

    def fill(p, r, n, uv, mv, gv):
        V0[p, pl.ds(r, n), :] = uv
        K[p, pl.ds(r, n), :] = lookup(mv)
        G[p, pl.ds(r, n), :] = gv.astype(jnp.float32)

    def blank(p, r, n):
        zero = jnp.zeros((n, lanes), jnp.float32)
        for ref in (V0, K, G):
            ref[p, pl.ds(r, n), :] = zero

    @pl.loop(0, depth)
    def _(p):
        fill(p + HALO, own0, rows, u_own[p], m_own[p], g_own[p])

    for side in range(2):
        r = R0 if side == 0 else own0 + rows
        @pl.when(comes_from[1][side])
        def _():
            for a in range(3):
                y_copy(side, a).wait_recv()
            for x_side in range(2):
                @pl.when(sends_to[0][x_side])
                def _():
                    for a in range(3):
                        c_copy(x_side, side, a).start()

            @pl.loop(0, depth)
            def _(p):
                fill(p + HALO, r, HALO, yu[side, p], ym[side, p], yg[side, p])
        @pl.when(jnp.logical_not(comes_from[1][side]))
        def _():
            @pl.loop(0, planes)
            def _(p):
                blank(p, r, HALO)

    for side in range(2):
        base = 0 if side == 0 else depth + HALO
        @pl.when(comes_from[0][side])
        def _():
            for j, a in x_parts(side):
                x_copy(side, j, a).wait_recv()

            @pl.loop(0, HALO)
            def _(j):
                fill(base + j, own0, rows, xu[side, j], xm[side, j], xg[side, j])

            for y_side in range(2):
                r = R0 if y_side == 0 else own0 + rows
                @pl.when(comes_from[1][y_side])
                def _():
                    for a in range(3):
                        c_copy(side, y_side, a).wait_recv()

                    @pl.loop(0, HALO)
                    def _(j):
                        fill(base + j, r, HALO, cu[side, y_side, j], cm[side, y_side, j], cg[side, y_side, j])
        @pl.when(jnp.logical_not(comes_from[0][side]))
        def _():
            @pl.loop(0, HALO)
            def _(j):
                blank(base + j, R0, ext)
            near = HALO - 1 if side == 0 else HALO + depth
            zero = jnp.zeros((ext, lanes), jnp.float32)
            for ref in (V1, V2, V3, Z3, Z2, Z1):
                ref[near, pl.ds(R0, ext), :] = zero

    lane = lax.broadcasted_iota(jnp.int32, (ext, lanes), 1)
    row = lax.broadcasted_iota(jnp.int32, (ext, lanes), 0)
    inside = jnp.where(
        jnp.logical_and(
            jnp.logical_or(row >= HALO, has_down),
            jnp.logical_or(row < HALO + rows, has_up),
        ), 1.0, 0.0).astype(jnp.float32)
    mid, low, high = pl.ds(R0, ext), pl.ds(R0 - 1, ext), pl.ds(R0 + 1, ext)

    @pl.loop(0, planes - 1)
    def _(p):
        WX[p, mid, :] = K[p, mid, :] + K[p + 1, mid, :]

    @pl.loop(1, planes - 1)
    def _(p):
        k = K[p, mid, :]
        above = jnp.where(lane == lanes - 1, 0.0, pltpu.roll(k, lanes - 1, 1))
        below = jnp.where(lane == 0, 0.0, pltpu.roll(k, 1, 1))
        k2 = k + k
        WY[p, mid, :] = k + K[p, high, :]
        WZ[p, mid, :] = jnp.where(lane == lanes - 1, 0.0, k + above)
        C[p, mid, :] = (WX[p, mid, :] + WX[p - 1, mid, :] + (k2 + (K[p, low, :] + K[p, high, :]))
                        + (k2 + (above + below)))

    def spread(src, p):
        v = src[p, mid, :]
        wz = WZ[p, mid, :]
        return v, (
            (WX[p, mid, :] * src[p + 1, mid, :] + WX[p - 1, mid, :] * src[p - 1, mid, :])
            + (WY[p, mid, :] * src[p, high, :] + WY[p, low, :] * src[p, low, :])
            + (wz * pltpu.roll(v, lanes - 1, 1) + pltpu.roll(wz * v, 1, 1))
            - C[p, mid, :] * v
        )

    def bounds(n):
        return (jnp.where(has_left, n, HALO), jnp.where(has_right, planes - n, planes - HALO))

    first, last = bounds(1)

    @pl.loop(first, last)
    def _(p):
        Z3[p, mid, :] = inside * (G[p, mid, :] * WX[p, mid, :] - G[p - 1, mid, :] * WX[p - 1, mid, :])

    for n, (src, dst, zsrc, zdst) in enumerate(((V0, V1, None, None), (V1, V2, Z3, Z2), (V2, V3, Z2, Z1))):
        first, last = bounds(n + 1)

        @pl.loop(first, last)
        def _(p):
            dst[p, mid, :] = inside * spread(src, p)[1]
            if zsrc is not None:
                v, d = spread(zsrc, p)
                zdst[p, mid, :] = v + inside * d

    own = pl.ds(own0, rows)
    own_low, own_high = pl.ds(own0 - 1, rows), pl.ds(own0 + 1, rows)
    own_lane = lax.broadcasted_iota(jnp.int32, (rows, lanes), 1)

    @pl.loop(HALO, HALO + depth)
    def _(p):
        v, d = spread(Z1, p)
        T[3, mid, :] = v + d
        e3 = spread(V3, p)[1]
        T[4, mid, :] = e3
        for i, z in enumerate((Z1, Z2, Z3)):
            T[i, mid, :] = z[p - 1, mid, :] + z[p, mid, :] + z[p + 1, mid, :]
        q = []
        for i, z in enumerate((Z1, Z2, Z3)):
            s = T[i, own_low, :] + T[i, own, :] + T[i, own_high, :]
            s = s + jnp.where(own_lane == lanes - 1, 0.0, pltpu.roll(s, lanes - 1, 1)) + jnp.where(
                own_lane == 0, 0.0, pltpu.roll(s, 1, 1))
            q.append(s * (1.0 / 27.0) - z[p, own, :])
        e1, e2 = V2[p, own, :], V3[p, own, :]
        r1 = e1 + e2
        r2 = r1 + e2 + T[4, own, :]
        ind_out[p - HALO] = (e1 * q[0] + r1 * q[1] + r2 * q[2]) * (-1.0 / (step_size * step_size))
        sens_out[p - HALO] = T[3, own, :] * (1.0 / step_size)

    for side in range(2):
        @pl.when(sends_to[1][side])
        def _():
            for a in range(3):
                y_copy(side, a).wait_send()
        @pl.when(sends_to[0][side])
        def _():
            for j, a in x_parts(side):
                x_copy(side, j, a).wait_send()
            for y_side in range(2):
                @pl.when(comes_from[1][y_side])
                def _():
                    for a in range(3):
                        c_copy(side, y_side, a).wait_send()


def solution(mesh):
    nx, ny = mesh.shape["gx"], mesh.shape["gy"]

    def step(initial, material, goal_faces, conductivity):
        depth, rows, lanes = initial.shape
        planes, tall = depth + 2 * HALO, rows + 2 * HALO + 16
        f32, i32 = jnp.float32, jnp.int32
        by_rows = (depth, rows // HALO, HALO, lanes)
        halos = []
        for shape in ((2, HALO, rows, lanes), (2, depth, HALO, lanes), (2, 2, HALO, HALO, lanes)):
            halos += [pltpu.VMEM(shape, t) for t in (f32, i32, i32)]
        sem = pltpu.SemaphoreType.DMA
        whole = pl.BlockSpec(memory_space=pltpu.MemorySpace.HBM)
        inside = pl.BlockSpec(memory_space=pltpu.VMEM)
        return pl.pallas_call(
            functools.partial(kernel, nx, ny),
            out_shape=[jax.ShapeDtypeStruct(initial.shape, f32)] * 2,
            in_specs=[whole] * 7,
            out_specs=[inside, inside],
            scratch_shapes=[pltpu.VMEM((depth, rows, lanes), t) for t in (f32, i32, i32)]
            + halos
            + [pltpu.VMEM((planes, tall, lanes), f32) for _ in range(13)]
            + [pltpu.VMEM((5, tall, lanes), f32)]
            + [pltpu.SMEM(conductivity.shape, f32), sem((4,)), sem((2, HALO, 3)), sem((2, HALO, 3)), sem((2, 3)), sem((2, 3)),
               sem((2, 2, 3)), sem((2, 2, 3))],
            compiler_params=pltpu.CompilerParams(collective_id=0, has_side_effects=True),
        )(conductivity, initial, material, goal_faces,
          initial.reshape(by_rows), material.reshape(by_rows), goal_faces.reshape(by_rows))

    placed = P("gx", "gy", None)
    return jax.shard_map(
        step,
        mesh=mesh,
        in_specs=(placed, placed, placed, P()),
        out_specs=(placed, placed),
        check_vma=False,
    )
```

time: 151 us -> 30.1 us (0.20)
  the two profiles are of different devices: /device:TPU:240 before, /device:TPU:1 now
where the time goes in v1:
time: 30.1 us; the launch traced here: 29.9 us
  Pallas kernels  26.6 us (88%)
  local copies, waits for them, and re-layouts  2.74 us (9%)
  between operations  0.65 us (2%)
    pallas_call x1, Pallas kernels, step(): pl.pallas_call(functools.partial(kernel, nx, ny), out_shape=[jax.ShapeDty...  26.6 us
    unnamed x4, local copies, waits for them, and re-layouts  2.74 us

profile of v1, /device:TPU:1, one launch (start us, length us, event | category | flops | bytes accessed | tf_op | source)
XLA Modules:
  0.0 29.9 jit_solution(18166244305810116523)
XLA Ops:
  0.6 26.6 %shard_map.59 = (f32[16,64,128]{2,1,0:T(8,128)}, f32[16,64,128]{2,1,0:T(8,128)}) custom-call(f32[8]{0:T(128)} %cond_in.1, f32[16,64,128]{2,1,0:T(8,128)} %u_in.1, s32[16,64,128]{2,1,0:T(8,128)} %m_in.1, s32[16,64,128]{2,1,0:T(8,128)} %g_in.1, f32[16,16,4,128]{3,2,1,0:T(4,128)} %bitcast.3, s32[16,16,4,128]{3,2,1,0:T(4,128)} %bitcast.4, s32[16,16,4,128]{3,2,1,0:T(4,128)} %bitcast.5), custom_call_target="tpu_custom_call" | custom-call | tf_op jit(solution)/shard_map/pallas_call | solution.py:279
  27.2 0.0 copy-start
  27.2 1.9 %copy.8 = f32[16,64,128]{2,1,0:T(8,128)} copy(f32[16,64,128]{2,1,0:T(8,128)} %get-tuple-element.4) | data formatting | bytes 1048576
  29.1 0.0 copy-done
  29.2 0.8 %copy.9 = f32[16,64,128]{2,1,0:T(8,128)} copy(f32[16,64,128]{2,1,0:T(8,128)S(1)} %copy-done) | data formatting | bytes 1048576
Async XLA Ops:
  27.2 2.0 %copy-start = (f32[16,64,128]{2,1,0:T(8,128)S(1)}, f32[16,64,128]{2,1,0:T(8,128)}, u32[]{:S(2)}) copy-start(f32[16,64,128]{2,1,0:T(8,128)} %get-tuple-element.5) | copy-start | bytes 1572868

commit v2 on v1

v2 whole, which is shorter than its diff:
```python
import functools

import jax
import jax.numpy as jnp
from jax import lax
from jax.experimental import pallas as pl
from jax.experimental.pallas import tpu as pltpu
from jax.sharding import PartitionSpec as P

MESH = pl.DeviceIdType.MESH
step_size = 0.075
HALO = 4
R0 = 8
CHUNK = 8


def kernel(
    nx, ny, cond_in,
    u_in, m_in, g_in, u_rows, m_rows, g_rows,
    ind_out, sens_out,
    u_own, m_own, g_own, xu, xm, xg, yu, ym, yg, cu, cm, cg,
    K, WX, WY, WZ, WB, C, G, V0, V1, V2, V3, Z3, Z2, Z1, S3, S2, M, T,
    cond, load_sem, x_send, x_recv, y_send, y_recv, c_send, c_recv,
):
    depth, rows, lanes = u_in.shape
    planes = depth + 2 * HALO
    ext = rows + 2 * HALO
    own0 = R0 + HALO
    gx, gy = lax.axis_index("gx"), lax.axis_index("gy")
    has_left, has_right = gx > 0, gx < nx - 1
    has_down, has_up = gy > 0, gy < ny - 1
    left, right = (gx - 1, gy), (gx + 1, gy)
    down, up = (gx, gy - 1), (gx, gy + 1)
    odd = lax.rem(gx, 2)

    barrier = pltpu.get_barrier_semaphore()
    sides = ((has_left, left), (has_right, right), (has_down, down), (has_up, up))
    for there, who in sides:
        @pl.when(there)
        def _():
            pl.semaphore_signal(barrier, inc=1, device_id=who, device_id_type=MESH)

    loads = [
        pltpu.make_async_copy(src, dst, load_sem.at[i])
        for i, (src, dst) in enumerate(((cond_in, cond), (m_in, m_own), (u_in, u_own), (g_in, g_own)))
    ]
    for load in loads:
        load.start()

    ins = (u_in, m_in, g_in)
    in_rows = (u_rows, m_rows, g_rows)
    xs, ys, cs = (xu, xm, xg), (yu, ym, yg), (cu, cm, cg)

    def remote(src, dst, send, recv, who):
        return pltpu.make_async_remote_copy(
            src_ref=src, dst_ref=dst, send_sem=send, recv_sem=recv,
            device_id=who, device_id_type=MESH,
        )

    def y_copy(side, a):
        who = up if side == 0 else down
        group = in_rows[a].shape[1] - 1 if side == 0 else 0
        return remote(in_rows[a].at[:, group], ys[a].at[side],
                      y_send.at[side, a], y_recv.at[side, a], who)

    def x_copy(side, j, a):
        who = right if side == 0 else left
        plane = depth - HALO + j if side == 0 else j
        return remote(ins[a].at[plane], xs[a].at[side, j],
                      x_send.at[side, j, a], x_recv.at[side, j, a], who)

    def c_copy(side, y_side, a):
        who = right if side == 0 else left
        first = depth - HALO if side == 0 else 0
        return remote(ys[a].at[y_side, pl.ds(first, HALO)], cs[a].at[side, y_side],
                      c_send.at[side, y_side, a], c_recv.at[side, y_side, a], who)

    sends_to = ((has_right, has_left), (has_up, has_down))
    comes_from = ((has_left, has_right), (has_down, has_up))

    def x_parts(side):
        order = (3, 2, 1, 0) if side == 0 else (0, 1, 2, 3)
        return [(j, a) for j in order for a in (1, 0, 2) if not (side == 1 and j == 3 and a == 2)]

    def lane_is(which, n):
        return lax.broadcasted_iota(jnp.int32, (n, lanes), 1) == which

    def turned(v):
        return pltpu.roll(v, lanes - 1, 1), pltpu.roll(v, 1, 1)

    def ends_off(a, b):
        n = a.shape[0]
        return jnp.where(lane_is(lanes - 1, n), 0.0, a), jnp.where(lane_is(0, n), 0.0, b)

    def chunks(r, n):
        while n > 0:
            yield r, min(n, CHUNK)
            r, n = r + CHUNK, n - CHUNK

    def fill(p, r, n, read):
        for i in range(0, n, CHUNK):
            m = min(CHUNK, n - i)
            uv, mv, gv = read(i, m)
            at = pl.ds(r + i, m)
            k = jnp.full(mv.shape, table[0], jnp.float32)
            for w in range(1, len(table)):
                k = jnp.where(mv == w, table[w], k)
            K[p, at, :] = k
            V0[p, at, :] = uv
            G[p, at, :] = gv.astype(jnp.float32)

    def blank(p, r, n):
        zero = jnp.zeros((n, lanes), jnp.float32)
        for ref in (V0, K, G):
            ref[p, pl.ds(r, n), :] = zero

    def faces_x(p, r, n):
        for s, m in chunks(r, n):
            at = pl.ds(s, m)
            WX[p, at, :] = K[p, at, :] + K[p + 1, at, :]

    def faces(p, r, n):
        for s, m in chunks(r, n):
            at, lo, hi = pl.ds(s, m), pl.ds(s - 1, m), pl.ds(s + 1, m)
            k = K[p, at, :]
            a, b = ends_off(*turned(k))
            h = K[p, hi, :]
            k2 = k + k
            WY[p, at, :] = k + h
            WZ[p, at, :] = jnp.where(lane_is(lanes - 1, m), 0.0, k + a)
            WB[p, at, :] = jnp.where(lane_is(0, m), 0.0, k + b)
            C[p, at, :] = ((WX[p, at, :] + WX[p - 1, at, :]) + (k2 + (K[p, lo, :] + h))) + (k2 + (a + b))

    def start_z(p, r, n, mask=None):
        for s, m in chunks(r, n):
            at = pl.ds(s, m)
            z = G[p, at, :] * WX[p, at, :] - G[p - 1, at, :] * WX[p - 1, at, :]
            Z3[p, at, :] = z if mask is None else z * mask(s, m)

    def spread(src, p, s, m):
        at, lo, hi = pl.ds(s, m), pl.ds(s - 1, m), pl.ds(s + 1, m)
        v = src[p, at, :]
        a, b = turned(v)
        d = (
            (WX[p, at, :] * src[p + 1, at, :] + WX[p - 1, at, :] * src[p - 1, at, :])
            + (WY[p, at, :] * src[p, hi, :] + WY[p, lo, :] * src[p, lo, :])
            + (WZ[p, at, :] * a + WB[p, at, :] * b)
            - C[p, at, :] * v
        )
        return v, a, b, d

    def forward(n, p, r, k, mask=None):
        src, dst = ((V0, V1), (V1, V2), (V2, V3))[n]
        for s, m in chunks(r, k):
            d = spread(src, p, s, m)[3]
            dst[p, pl.ds(s, m), :] = d if mask is None else d * mask(s, m)

    def backward(n, p, r, k, mask=None):
        src, dst, box = (None, (Z3, Z2, S3), (Z2, Z1, S2))[n]
        for s, m in chunks(r, k):
            v, a, b, d = spread(src, p, s, m)
            at = pl.ds(s, m)
            dst[p, at, :] = v + (d if mask is None else d * mask(s, m))
            a, b = ends_off(a, b)
            box[p, at, :] = v + (a + b)

    def finish(p):
        for i, z in enumerate((Z1, S2, S3)):
            for s, m in chunks(own0 - 1, rows + 2):
                at = pl.ds(s, m)
                T[i, at, :] = z[p - 1, at, :] + z[p, at, :] + z[p + 1, at, :]
        for s, m in chunks(own0, rows):
            at, lo, hi = pl.ds(s, m), pl.ds(s - 1, m), pl.ds(s + 1, m)
            e1, e2, e3 = V2[p, at, :], V3[p, at, :], spread(V3, p, s, m)[3]
            z1, _, _, d = spread(Z1, p, s, m)
            r1 = e1 + e2
            r2 = r1 + (e2 + e3)
            sums = [T[i, lo, :] + T[i, at, :] + T[i, hi, :] for i in range(3)]
            a, b = ends_off(*turned(sums[0]))
            q1 = sums[0] + (a + b)
            third = 1.0 / 27.0
            total = (e1 * (q1 * third - z1) + r1 * (sums[1] * third - Z2[p, at, :])
                     + r2 * (sums[2] * third - Z3[p, at, :]))
            out = pl.ds(s - own0, m)
            ind_out[p - HALO, out, :] = total * (-1.0 / (step_size * step_size))
            sens_out[p - HALO, out, :] = (z1 + d) * (1.0 / step_size)

    loads[0].wait()
    loads[1].wait()
    loads[2].wait()
    loads[3].wait()
    table = [cond[i] * (0.5 * step_size) for i in range(cond.shape[0])]
    row = lax.broadcasted_iota(jnp.int32, (ext, lanes), 0)
    M[pl.ds(R0, ext), :] = jnp.where(
        jnp.logical_and(
            jnp.logical_or(row >= HALO, has_down),
            jnp.logical_or(row < HALO + rows, has_up),
        ), 1.0, 0.0).astype(jnp.float32)

    pl.semaphore_wait(barrier, sum(there.astype(jnp.int32) for there, _ in sides))
    for side in range(2):
        @pl.when(sends_to[1][side])
        def _():
            for a in range(3):
                y_copy(side, a).start()
    for side in range(2):
        @pl.when(sends_to[0][side])
        def _():
            for j, a in x_parts(side):
                x_copy(side, j, a).start()

    @pl.loop(0, depth)
    def _(p):
        fill(p + HALO, own0, rows, lambda i, m: (
            u_own[p, pl.ds(i, m), :], m_own[p, pl.ds(i, m), :], g_own[p, pl.ds(i, m), :]))

    first, last = HALO + 1, HALO + depth - 1

    def each(lo, hi, body, unroll=2):
        @pl.loop(0, (hi - lo) // unroll)
        def _(i):
            for j in range(unroll):
                body(lo + i * unroll + j)

    @pl.loop(HALO, last)
    def _(p):
        faces_x(p, own0, rows)

    each(first, last, lambda p: (faces(p, own0, rows), start_z(p, own0, rows)))
    for n in range(3):
        def inner(p):
            forward(n, p, own0 + 1 + n, rows - 2 - 2 * n)
            if n:
                backward(n, p, own0 + 1 + n, rows - 2 - 2 * n)
        each(first + n, last - n, inner)

    for side in range(2):
        r = R0 if side == 0 else own0 + rows
        @pl.when(comes_from[1][side])
        def _():
            for a in range(3):
                y_copy(side, a).wait_recv()
            for x_side in range(2):
                @pl.when(sends_to[0][x_side])
                def _():
                    for a in range(3):
                        c_copy(x_side, side, a).start()

            @pl.loop(0, depth)
            def _(p):
                fill(p + HALO, r, HALO, lambda i, m: (yu[side, p], ym[side, p], yg[side, p]))
        @pl.when(jnp.logical_not(comes_from[1][side]))
        def _():
            @pl.loop(0, planes)
            def _(p):
                blank(p, r, HALO)

    def row_mask(s, m):
        return M[pl.ds(s, m), :]

    edge_tiles = (R0, own0 + rows - HALO)

    @pl.loop(HALO, last)
    def _(p):
        for r in edge_tiles:
            faces_x(p, r, 2 * HALO)

    def edges(p):
        for r in edge_tiles:
            faces(p, r, 2 * HALO)
            start_z(p, r, 2 * HALO, row_mask)
    each(first, last, edges)
    for n in range(3):
        def strip(p):
            for r in (R0 + 1 + n, own0 + rows - 1 - n):
                forward(n, p, r, HALO, row_mask)
                if n:
                    backward(n, p, r, HALO, row_mask)
        each(first + n, last - n, strip)
    each(2 * HALO, depth, finish, 1)

    @pl.loop(0, 2)
    def _(turn):
        high = lax.rem(odd + 1 + turn, 2)
        base = high * (depth + HALO)
        for side in range(2):
            @pl.when(high == side)
            def _():
                @pl.when(comes_from[0][side])
                def _():
                    for j, a in x_parts(side):
                        x_copy(side, j, a).wait_recv()
                    for y_side in range(2):
                        @pl.when(comes_from[1][y_side])
                        def _():
                            for a in range(3):
                                c_copy(side, y_side, a).wait_recv()

        there = jnp.where(high == 1, has_right, has_left)

        @pl.when(there)
        def _():
            @pl.loop(0, HALO)
            def _(j):
                fill(base + j, own0, rows, lambda i, m: (
                    xu[high, j, pl.ds(i, m), :], xm[high, j, pl.ds(i, m), :], xg[high, j, pl.ds(i, m), :]))
                for y_side in range(2):
                    @pl.when(comes_from[1][y_side])
                    def _():
                        fill(base + j, R0 if y_side == 0 else own0 + rows, HALO, lambda i, m: (
                            cu[high, y_side, j], cm[high, y_side, j], cg[high, y_side, j]))

        @pl.when(jnp.logical_not(there))
        def _():
            @pl.loop(0, HALO)
            def _(j):
                blank(base + j, R0, ext)

        @pl.loop(0, HALO)
        def _(j):
            faces_x(high * (depth + HALO - 1) + j, R0, ext)

        def plane_mask(p):
            inside = jnp.logical_or(there, jnp.logical_and(p >= HALO, p < HALO + depth))
            scale = jnp.where(inside, 1.0, 0.0).astype(jnp.float32)
            return lambda s, m: M[pl.ds(s, m), :] * scale

        def start(p):
            faces(p, R0, ext)
            start_z(p, R0, ext, plane_mask(p))

        lo = 1 + high * (depth + 2)
        each(lo, lo + HALO, start)
        for n in range(3):
            def shell(p):
                forward(n, p, R0 + 1 + n, ext - 2 - 2 * n, plane_mask(p))
                if n:
                    backward(n, p, R0 + 1 + n, ext - 2 - 2 * n, plane_mask(p))
            begin = lo + n - 2 * n * high
            each(begin, begin + HALO, shell)
        begin = HALO + high * (depth - HALO)
        each(begin, begin + HALO, finish, 1)

    for side in range(2):
        @pl.when(sends_to[1][side])
        def _():
            for a in range(3):
                y_copy(side, a).wait_send()
        @pl.when(sends_to[0][side])
        def _():
            for j, a in x_parts(side):
                x_copy(side, j, a).wait_send()
            for y_side in range(2):
                @pl.when(comes_from[1][y_side])
                def _():
                    for a in range(3):
                        c_copy(side, y_side, a).wait_send()


def put_out(a, b, a_out, b_out, sem):
    part = a.shape[0] // 4
    copies = [
        pltpu.make_async_copy(src.at[pl.ds(q * part, part)], dst.at[pl.ds(q * part, part)], sem.at[i, q])
        for i, (src, dst) in enumerate(((a, a_out), (b, b_out))) for q in range(4)
    ]
    for copy in copies:
        copy.start()
    for copy in copies:
        copy.wait()


def solution(mesh):
    nx, ny = mesh.shape["gx"], mesh.shape["gy"]

    def step(initial, material, goal_faces, conductivity):
        depth, rows, lanes = initial.shape
        planes, tall = depth + 2 * HALO, rows + 2 * HALO + 16
        f32, i32 = jnp.float32, jnp.int32
        by_rows = (depth, rows // HALO, HALO, lanes)
        halos = []
        for shape in ((2, HALO, rows, lanes), (2, depth, HALO, lanes), (2, 2, HALO, HALO, lanes)):
            halos += [pltpu.VMEM(shape, t) for t in (f32, i32, i32)]
        sem = pltpu.SemaphoreType.DMA
        whole = pl.BlockSpec(memory_space=pltpu.MemorySpace.HBM)
        inside = pl.BlockSpec(memory_space=pltpu.VMEM)

        def keep(v):
            return pltpu.with_memory_space_constraint(v, pltpu.MemorySpace.HBM)

        args = (conductivity, initial, material, goal_faces,
                initial.reshape(by_rows), material.reshape(by_rows), goal_faces.reshape(by_rows))
        ind, sens = pl.pallas_call(
            functools.partial(kernel, nx, ny),
            out_shape=[pltpu.VMEM(initial.shape, f32)] * 2,
            in_specs=[whole] * 7,
            out_specs=[inside, inside],
            scratch_shapes=[pltpu.VMEM((depth, rows, lanes), t) for t in (f32, i32, i32)]
            + halos
            + [pltpu.VMEM((planes, tall, lanes), f32) for _ in range(16)]
            + [pltpu.VMEM((tall, lanes), f32), pltpu.VMEM((3, tall, lanes), f32)]
            + [pltpu.SMEM(conductivity.shape, f32), sem((4,)), sem((2, HALO, 3)), sem((2, HALO, 3)),
               sem((2, 3)), sem((2, 3)), sem((2, 2, 3)), sem((2, 2, 3))],
            compiler_params=pltpu.CompilerParams(
                collective_id=0, has_side_effects=True, vmem_limit_bytes=50 << 20),
            name="cells",
        )(*(keep(v) for v in args))
        return pl.pallas_call(
            put_out,
            out_shape=[jax.ShapeDtypeStruct(initial.shape, f32)] * 2,
            in_specs=[inside] * 2,
            out_specs=[pl.BlockSpec(memory_space=pl.ANY)] * 2,
            scratch_shapes=[sem((2, 4))],
            compiler_params=pltpu.CompilerParams(vmem_limit_bytes=4 << 20),
            name="put_out",
        )(ind, sens)

    placed = P("gx", "gy", None)
    return jax.shard_map(
        step,
        mesh=mesh,
        in_specs=(placed, placed, placed, P()),
        out_specs=(placed, placed),
        check_vma=False,
    )
```

time: 30.1 us -> 21 us (0.70)
  Pallas kernels: 26.6 us -> 20.3 us
  local copies, waits for them, and re-layouts: 2.74 us -> 0 us
    pallas_call x1 -> x2, Pallas kernels: 26.6 us -> 20.3 us  [the longest x1 19.2 us: step(): pl.pallas_call(functools.partial(kernel, nx, ny), out_shape=[pltpu.VMEM(i...]
    unnamed x4 -> x0, local copies, waits for them, and re-layouts: 2.74 us -> none
where the time goes in v2:
time: 21 us; the launch traced here: 20.9 us
  Pallas kernels  20.3 us (97%)
  between operations  0.64 us (3%)
    pallas_call x1, Pallas kernels, step(): pl.pallas_call(functools.partial(kernel, nx, ny), out_shape=[pltpu.VMEM(i...  19.2 us
    pallas_call x1, Pallas kernels, step(): pl.pallas_call(put_out, out_shape=[jax.ShapeDtypeStruct(initial.shape, f3...  1.03 us

profile of v2, /device:TPU:1, one launch (start us, length us, event | category | flops | bytes accessed | tf_op | source)
XLA Modules:
  0.0 20.9 jit_solution(7842770575103988032)
XLA Ops:
  0.6 19.2 %cells.1 = (f32[16,64,128]{2,1,0:T(8,128)S(1)}, f32[16,64,128]{2,1,0:T(8,128)S(1)}) custom-call(f32[8]{0:T(128)} %cond_in.1, f32[16,64,128]{2,1,0:T(8,128)} %u_in.1, s32[16,64,128]{2,1,0:T(8,128)} %m_in.1, s32[16,64,128]{2,1,0:T(8,128)} %g_in.1, f32[16,16,4,128]{3,2,1,0:T(4,128)} %bitcast.3, s32[16,16,4,128]{3,2,1,0:T(4,128)} %bitcast.4, ...), custom_call_target="tpu_custom_call" | custom-call | tf_op jit(solution)/shard_map/cells/pallas_call | solution.py:392
  19.9 1.0 %put_out.1 = (f32[16,64,128]{2,1,0:T(8,128)}, f32[16,64,128]{2,1,0:T(8,128)}) custom-call(f32[16,64,128]{2,1,0:T(8,128)S(1)} %get-tuple-element.4.a, f32[16,64,128]{2,1,0:T(8,128)S(1)} %get-tuple-element.5.b), custom_call_target="tpu_custom_call" | custom-call | tf_op jit(solution)/shard_map/put_out/pallas_call | solution.py:407

commit v3 on v2

--- a/solution.py
+++ b/solution.py
@@ -18,9 +18,9 @@
     nx, ny, cond_in,
     u_in, m_in, g_in, u_rows, m_rows, g_rows,
     ind_out, sens_out,
-    u_own, m_own, g_own, xu, xm, xg, yu, ym, yg, cu, cm, cg,
+    u_own, m_own, g_own, xu, xm, xg, yu, ym, yg, cu, cm, cg, eu, em, eg,
     K, WX, WY, WZ, WB, C, G, V0, V1, V2, V3, Z3, Z2, Z1, S3, S2, M, T,
-    cond, load_sem, x_send, x_recv, y_send, y_recv, c_send, c_recv,
+    cond, load_sem, x_send, x_recv, y_send, y_recv, c_send, c_recv, e_send, e_recv, late,
 ):
     depth, rows, lanes = u_in.shape
     planes = depth + 2 * HALO
@@ -33,10 +33,19 @@
     down, up = (gx, gy - 1), (gx, gy + 1)
     odd = lax.rem(gx, 2)
 
+    both, either = jnp.logical_and, jnp.logical_or
+    is_first = both(gx == 0, gy == 0)
+    beside_x, beside_y = both(gx == 1, gy == 0), both(gx == 0, gy == 1)
+    across = both(gx == 1, gy == 1)
+    beside = either(beside_x, beside_y)
+
+    def unless(cond, but):
+        return both(cond, jnp.logical_not(but))
+
     barrier = pltpu.get_barrier_semaphore()
     sides = ((has_left, left), (has_right, right), (has_down, down), (has_up, up))
     for there, who in sides:
-        @pl.when(there)
+        @pl.when(unless(there, is_first))
         def _():
             pl.semaphore_signal(barrier, inc=1, device_id=who, device_id_type=MESH)
 
@@ -57,11 +66,23 @@
             device_id=who, device_id_type=MESH,
         )
 
-    def y_copy(side, a):
+    y_parts = ((0, HALO), (depth - HALO, HALO), (HALO, depth - 2 * HALO))
+
+    def y_copy(side, part, a):
         who = up if side == 0 else down
         group = in_rows[a].shape[1] - 1 if side == 0 else 0
-        return remote(in_rows[a].at[:, group], ys[a].at[side],
-                      y_send.at[side, a], y_recv.at[side, a], who)
+        at = pl.ds(*y_parts[part])
+        return remote(in_rows[a].at[at, group], ys[a].at[side, at],
+                      y_send.at[side, part, a], y_recv.at[side, part, a], who)
+
+    def y_start(side):
+        for part in range(3):
+            for a in range(3):
+                y_copy(side, part, a).start()
+
+    def x_start(side):
+        for j, a in x_parts(side):
+            x_copy(side, j, a).start()
 
     def x_copy(side, j, a):
         who = right if side == 0 else left
@@ -75,8 +96,20 @@
         return remote(ys[a].at[y_side, pl.ds(first, HALO)], cs[a].at[side, y_side],
                       c_send.at[side, y_side, a], c_recv.at[side, y_side, a], who)
 
+    def e_copy(a):
+        return remote(xs[a].at[0, :, pl.ds(0, 2 * HALO)], (eu, em, eg)[a],
+                      e_send.at[a], e_recv.at[a], down)
+
     sends_to = ((has_right, has_left), (has_up, has_down))
     comes_from = ((has_left, has_right), (has_down, has_up))
+
+    def c_sent(x_side, y_side):
+        there = sends_to[0][x_side]
+        return unless(there, is_first) if (x_side, y_side) == (0, 1) else there
+
+    def c_now(x_side, y_side):
+        there = c_sent(x_side, y_side)
+        return unless(there, beside_x) if x_side == 1 else there
 
     def x_parts(side):
         order = (3, 2, 1, 0) if side == 0 else (0, 1, 2, 3)
@@ -197,17 +230,21 @@
             jnp.logical_or(row < HALO + rows, has_up),
         ), 1.0, 0.0).astype(jnp.float32)
 
-    pl.semaphore_wait(barrier, sum(there.astype(jnp.int32) for there, _ in sides))
+    pl.semaphore_wait(barrier, sum(there.astype(jnp.int32) for there, _ in sides) - beside.astype(jnp.int32))
+
+    @pl.when(is_first)
+    def _():
+        for who in (right, up):
+            pl.semaphore_signal(late, inc=1, device_id=who, device_id_type=MESH)
+
     for side in range(2):
-        @pl.when(sends_to[1][side])
-        def _():
-            for a in range(3):
-                y_copy(side, a).start()
+        @pl.when(unless(sends_to[1][side], beside_y) if side else sends_to[1][side])
+        def _():
+            y_start(side)
     for side in range(2):
-        @pl.when(sends_to[0][side])
-        def _():
-            for j, a in x_parts(side):
-                x_copy(side, j, a).start()
+        @pl.when(unless(sends_to[0][side], beside_x) if side else sends_to[0][side])
+        def _():
+            x_start(side)
 
     @pl.loop(0, depth)
     def _(p):
@@ -234,17 +271,35 @@
                 backward(n, p, own0 + 1 + n, rows - 2 - 2 * n)
         each(first + n, last - n, inner)
 
+    @pl.when(beside_y)
+    def _():
+        pl.semaphore_wait(late, 1)
+        y_start(1)
+
+    @pl.when(across)
+    def _():
+        for j, a in x_parts(0):
+            x_copy(0, j, a).wait_recv()
+        for a in range(3):
+            e_copy(a).start()
+
+    for side in range(2):
+        @pl.when(comes_from[1][side])
+        def _():
+            for part in range(2):
+                for a in range(3):
+                    y_copy(side, part, a).wait_recv()
+            for x_side in range(2):
+                @pl.when(c_now(x_side, side))
+                def _():
+                    for a in range(3):
+                        c_copy(x_side, side, a).start()
     for side in range(2):
         r = R0 if side == 0 else own0 + rows
         @pl.when(comes_from[1][side])
         def _():
             for a in range(3):
-                y_copy(side, a).wait_recv()
-            for x_side in range(2):
-                @pl.when(sends_to[0][x_side])
-                def _():
-                    for a in range(3):
-                        c_copy(x_side, side, a).start()
+                y_copy(side, 2, a).wait_recv()
 
             @pl.loop(0, depth)
             def _(p):
@@ -277,6 +332,14 @@
                 if n:
                     backward(n, p, r, HALO, row_mask)
         each(first + n, last - n, strip)
+
+    @pl.when(beside_x)
+    def _():
+        pl.semaphore_wait(late, 1)
+        x_start(1)
+        for a in range(3):
+            c_copy(1, 1, a).start()
+
     each(2 * HALO, depth, finish, 1)
 
     @pl.loop(0, 2)
@@ -286,12 +349,24 @@
         for side in range(2):
             @pl.when(high == side)
             def _():
-                @pl.when(comes_from[0][side])
+                @pl.when(comes_from[0][side] if side else unless(comes_from[0][side], across))
                 def _():
                     for j, a in x_parts(side):
                         x_copy(side, j, a).wait_recv()
+
+                @pl.when(comes_from[0][side])
+                def _():
                     for y_side in range(2):
-                        @pl.when(comes_from[1][y_side])
+                        there = comes_from[1][y_side]
+                        if (side, y_side) == (0, 1):
+                            there = unless(there, beside_x)
+
+                            @pl.when(beside_x)
+                            def _():
+                                for a in range(3):
+                                    e_copy(a).wait_recv()
+
+                        @pl.when(there)
                         def _():
                             for a in range(3):
                                 c_copy(side, y_side, a).wait_recv()
@@ -304,8 +379,15 @@
             def _(j):
                 fill(base + j, own0, rows, lambda i, m: (
                     xu[high, j, pl.ds(i, m), :], xm[high, j, pl.ds(i, m), :], xg[high, j, pl.ds(i, m), :]))
+                other_way = both(beside_x, high == 0)
+
+                @pl.when(other_way)
+                def _():
+                    fill(base + j, own0 + rows, HALO, lambda i, m: (
+                        eu[j, pl.ds(0, HALO), :], em[j, pl.ds(0, HALO), :], eg[j, pl.ds(0, HALO), :]))
+
                 for y_side in range(2):
-                    @pl.when(comes_from[1][y_side])
+                    @pl.when(unless(comes_from[1][y_side], other_way) if y_side else comes_from[1][y_side])
                     def _():
                         fill(base + j, R0 if y_side == 0 else own0 + rows, HALO, lambda i, m: (
                             cu[high, y_side, j], cm[high, y_side, j], cg[high, y_side, j]))
@@ -344,17 +426,23 @@
     for side in range(2):
         @pl.when(sends_to[1][side])
         def _():
-            for a in range(3):
-                y_copy(side, a).wait_send()
+            for part in range(3):
+                for a in range(3):
+                    y_copy(side, part, a).wait_send()
         @pl.when(sends_to[0][side])
         def _():
             for j, a in x_parts(side):
                 x_copy(side, j, a).wait_send()
-            for y_side in range(2):
-                @pl.when(comes_from[1][y_side])
-                def _():
-                    for a in range(3):
-                        c_copy(side, y_side, a).wait_send()
+        for y_side in range(2):
+            @pl.when(both(comes_from[1][y_side], c_sent(side, y_side)))
+            def _():
+                for a in range(3):
+                    c_copy(side, y_side, a).wait_send()
+
+    @pl.when(across)
+    def _():
+        for a in range(3):
+            e_copy(a).wait_send()
 
 
 def put_out(a, b, a_out, b_out, sem):
@@ -378,7 +466,8 @@
         f32, i32 = jnp.float32, jnp.int32
         by_rows = (depth, rows // HALO, HALO, lanes)
         halos = []
-        for shape in ((2, HALO, rows, lanes), (2, depth, HALO, lanes), (2, 2, HALO, HALO, lanes)):
+        for shape in ((2, HALO, rows, lanes), (2, depth, HALO, lanes), (2, 2, HALO, HALO, lanes),
+                      (HALO, 2 * HALO, lanes)):
             halos += [pltpu.VMEM(shape, t) for t in (f32, i32, i32)]
         sem = pltpu.SemaphoreType.DMA
         whole = pl.BlockSpec(memory_space=pltpu.MemorySpace.HBM)
@@ -399,7 +488,8 @@
             + [pltpu.VMEM((planes, tall, lanes), f32) for _ in range(16)]
             + [pltpu.VMEM((tall, lanes), f32), pltpu.VMEM((3, tall, lanes), f32)]
             + [pltpu.SMEM(conductivity.shape, f32), sem((4,)), sem((2, HALO, 3)), sem((2, HALO, 3)),
-               sem((2, 3)), sem((2, 3)), sem((2, 2, 3)), sem((2, 2, 3))],
+               sem((2, 3, 3)), sem((2, 3, 3)), sem((2, 2, 3)), sem((2, 2, 3)), sem((3,)), sem((3,)),
+               pltpu.SemaphoreType.REGULAR],
             compiler_params=pltpu.CompilerParams(
                 collective_id=0, has_side_effects=True, vmem_limit_bytes=50 << 20),
             name="cells",

time: 21 us -> 20.5 us (0.976)
  the two profiles are of different devices: /device:TPU:1 before, /device:TPU:32 now
where the time goes in v3:
time: 20.5 us; the launch traced here: 20.4 us
  Pallas kernels  19.8 us (97%)
  between operations  0.64 us (3%)
    pallas_call x1, Pallas kernels, step(): pl.pallas_call(functools.partial(kernel, nx, ny), out_shape=[pltpu.VMEM(i...  18.7 us
    pallas_call x1, Pallas kernels, step(): pl.pallas_call(put_out, out_shape=[jax.ShapeDtypeStruct(initial.shape, f3...  1.03 us

profile of v3, /device:TPU:32, one launch (start us, length us, event | category | flops | bytes accessed | tf_op | source)
XLA Modules:
  0.0 20.4 jit_solution(16970082367079520488)
XLA Ops:
  0.6 18.7 %cells.1 = (f32[16,64,128]{2,1,0:T(8,128)S(1)}, f32[16,64,128]{2,1,0:T(8,128)S(1)}) custom-call(f32[8]{0:T(128)} %cond_in.1, f32[16,64,128]{2,1,0:T(8,128)} %u_in.1, s32[16,64,128]{2,1,0:T(8,128)} %m_in.1, s32[16,64,128]{2,1,0:T(8,128)} %g_in.1, f32[16,16,4,128]{3,2,1,0:T(4,128)} %bitcast.3, s32[16,16,4,128]{3,2,1,0:T(4,128)} %bitcast.4, ...), custom_call_target="tpu_custom_call" | custom-call | tf_op jit(solution)/shard_map/cells/pallas_call | solution.py:481
  19.4 1.0 %put_out.1 = (f32[16,64,128]{2,1,0:T(8,128)}, f32[16,64,128]{2,1,0:T(8,128)}) custom-call(f32[16,64,128]{2,1,0:T(8,128)S(1)} %get-tuple-element.4.a, f32[16,64,128]{2,1,0:T(8,128)S(1)} %get-tuple-element.5.b), custom_call_target="tpu_custom_call" | custom-call | tf_op jit(solution)/shard_map/put_out/pallas_call | solution.py:497

commit v4 on v2

v4 whole, which is shorter than its diff:
```python
import functools

import jax
import jax.numpy as jnp
from jax import lax
from jax.experimental import pallas as pl
from jax.experimental.pallas import tpu as pltpu
from jax.sharding import PartitionSpec as P

MESH = pl.DeviceIdType.MESH
step_size = 0.075
HALO = 4
R0 = 8
CHUNK = 8
FINISH = 2


def kernel(
    nx, ny, cond_in,
    u_in, m_in, g_in, u_rows, m_rows, g_rows,
    ind_out, sens_out,
    u_all, m_all, g_all, u_edge, m_edge, g_edge, eu, em, eg,
    K, WX, WY, WZ, WB, C, G, V0, V1, V2, V3, Z3, Z2, Z1, S3, S2, M, T,
    cond, load_sem, x_send, x_recv, y_send, y_recv, c_send, c_recv, e_send, e_recv, late,
):
    depth, rows, lanes = u_in.shape
    V, Z, S = (V0, V1, V2, V3), (Z3, Z2, Z1), (S3, S2)
    groups = u_rows.shape[1]
    ext = rows + 2 * HALO
    own0 = R0 + HALO
    gx, gy = lax.axis_index("gx"), lax.axis_index("gy")
    has_left, has_right = gx > 0, gx < nx - 1
    has_down, has_up = gy > 0, gy < ny - 1
    left, right = (gx - 1, gy), (gx + 1, gy)
    down, up = (gx, gy - 1), (gx, gy + 1)
    odd = lax.rem(gx, 2)

    both, either = jnp.logical_and, jnp.logical_or
    is_first = both(gx == 0, gy == 0)
    beside_x, beside_y = both(gx == 1, gy == 0), both(gx == 0, gy == 1)
    across = both(gx == 1, gy == 1)
    beside = either(beside_x, beside_y)

    def unless(cond, but):
        return both(cond, jnp.logical_not(but))

    barrier = pltpu.get_barrier_semaphore()
    sides = ((has_left, left), (has_right, right), (has_down, down), (has_up, up))
    for there, who in sides:
        @pl.when(unless(there, is_first))
        def _():
            pl.semaphore_signal(barrier, inc=1, device_id=who, device_id_type=MESH)

    own_planes = pl.ds(HALO, depth)
    loads = [
        pltpu.make_async_copy(src, dst, load_sem.at[i])
        for i, (src, dst) in enumerate((
            (cond_in, cond), (m_in, m_all.at[own_planes]), (u_in, u_all.at[own_planes]), (g_in, g_all.at[own_planes])))
    ]
    for load in loads:
        load.start()

    ins, in_rows = (u_in, m_in, g_in), (u_rows, m_rows, g_rows)
    alls, edges_of = (u_all, m_all, g_all), (u_edge, m_edge, g_edge)

    def remote(src, dst, send, recv, who):
        return pltpu.make_async_remote_copy(
            src_ref=src, dst_ref=dst, send_sem=send, recv_sem=recv,
            device_id=who, device_id_type=MESH,
        )

    def y_copies(side):
        who = (gx, gy + 1 - 2 * side)
        return [
            remote(in_rows[a].at[:, (1 - side) * (groups - 1)], edges_of[a].at[side, own_planes],
                   y_send.at[side, a], y_recv.at[side, a], who)
            for a in range(3)
        ]

    def x_copies(side):
        who = (gx + 1 - 2 * side, gy)
        first, place = (1 - side) * (depth - HALO), side * (depth + HALO)
        return [
            remote(ins[a].at[pl.ds(first + skip, n)], alls[a].at[pl.ds(place + skip, n)],
                   x_send.at[side, i], x_recv.at[side, i], who)
            for i, (a, skip, n) in enumerate(((1, 0, HALO), (0, 0, HALO), (2, 0, HALO - 1)))
        ]

    def x_last(side):
        who = (gx + 1 - 2 * side, gy)
        return remote(g_in.at[depth - 1], g_all.at[HALO - 1], x_send.at[0, 3], x_recv.at[0, 3], who)

    def c_copies(side, y_side):
        who = (gx + 1 - 2 * side, gy)
        first, place = HALO + (1 - side) * (depth - HALO), side * (depth + HALO)
        return [
            remote(edges_of[a].at[y_side, pl.ds(first, HALO)], edges_of[a].at[y_side, pl.ds(place, HALO)],
                   c_send.at[side, y_side, a], c_recv.at[side, y_side, a], who)
            for a in range(3)
        ]

    def e_copies():
        return [
            remote(alls[a].at[pl.ds(0, HALO), pl.ds(0, 2 * HALO)], (eu, em, eg)[a],
                   e_send.at[a], e_recv.at[a], down)
            for a in range(3)
        ]

    def pick(side, low, high):
        return either(both(side == 0, low), both(side == 1, high))

    def x_to(side):
        return pick(side, has_right, has_left)

    def x_from(side):
        return pick(side, has_left, has_right)

    def y_to(side):
        return pick(side, has_up, has_down)

    def y_from(side):
        return pick(side, has_down, has_up)

    def c_sent(side, y_side):
        way = unless(x_to(side), both(is_first, both(side == 0, y_side == 1)))
        return both(y_from(y_side), way)

    def start_all(copies):
        for copy in copies:
            copy.start()

    def x_start(side):
        start_all(x_copies(side))

        @pl.when(side == 0)
        def _():
            x_last(side).start()

    def x_arrive(side):
        for copy in x_copies(side):
            copy.wait_recv()

        @pl.when(side == 0)
        def _():
            x_last(side).wait_recv()

    def turned(v):
        return pltpu.roll(v, lanes - 1, 1), pltpu.roll(v, 1, 1)

    def lane_is(which, n):
        return lax.broadcasted_iota(jnp.int32, (n, lanes), 1) == which

    def ends_off(a, b):
        n = a.shape[0]
        return jnp.where(lane_is(lanes - 1, n), 0.0, a), jnp.where(lane_is(0, n), 0.0, b)

    def chunks(r, n):
        while n > 0:
            yield r, min(n, CHUNK)
            r, n = r + CHUNK, n - CHUNK

    def fill(p, r, n, there, read):
        for i in range(0, n, CHUNK):
            m = min(CHUNK, n - i)
            uv, mv, gv = read(i, m)
            at = pl.ds(r + i, m)
            k = jnp.full(mv.shape, table[0], jnp.float32)
            for w in range(1, len(table)):
                k = jnp.where(mv == w, table[w], k)
            K[p, at, :] = jnp.where(there, k, 0.0)
            V[0][p, at, :] = jnp.where(there, uv, 0.0)
            G[p, at, :] = jnp.where(there, gv.astype(jnp.float32), 0.0)

    def fill_own(p, there):
        fill(p, own0, rows, there, lambda i, m: tuple(ref[p, pl.ds(i, m), :] for ref in alls))

    def fill_edges(p, there):
        for side, r in ((0, R0), (1, own0 + rows)):
            fill(p, r, HALO, both(there, y_from(side)), lambda i, m: tuple(ref[side, p] for ref in edges_of))

    def faces_x(p, r, n):
        for s, m in chunks(r, n):
            at = pl.ds(s, m)
            WX[p, at, :] = K[p, at, :] + K[p + 1, at, :]

    def faces(p, r, n, scale):
        for s, m in chunks(r, n):
            at, lo, hi = pl.ds(s, m), pl.ds(s - 1, m), pl.ds(s + 1, m)
            k = K[p, at, :]
            a, b = ends_off(*turned(k))
            h = K[p, hi, :]
            k2 = k + k
            WY[p, at, :] = k + h
            WZ[p, at, :] = jnp.where(lane_is(lanes - 1, m), 0.0, k + a)
            WB[p, at, :] = jnp.where(lane_is(0, m), 0.0, k + b)
            wx, wx_low = WX[p, at, :], WX[p - 1, at, :]
            C[p, at, :] = ((wx + wx_low) + (k2 + (K[p, lo, :] + h))) + (k2 + (a + b))
            Z[0][p, at, :] = (G[p, at, :] * wx - G[p - 1, at, :] * wx_low) * (M[at, :] * scale)

    def spread(src, p, s, m):
        at, lo, hi = pl.ds(s, m), pl.ds(s - 1, m), pl.ds(s + 1, m)
        v = src[p, at, :]
        a, b = turned(v)
        d = (
            (WX[p, at, :] * src[p + 1, at, :] + WX[p - 1, at, :] * src[p - 1, at, :])
            + (WY[p, at, :] * src[p, hi, :] + WY[p, lo, :] * src[p, lo, :])
            + (WZ[p, at, :] * a + WB[p, at, :] * b)
            - C[p, at, :] * v
        )
        return v, a, b, d

    def forward(n, p, r, k, scale):
        for s, m in chunks(r, k):
            at = pl.ds(s, m)
            V[n + 1][p, at, :] = spread(V[n], p, s, m)[3] * (M[at, :] * scale)

    def backward(n, p, r, k, scale):
        for s, m in chunks(r, k):
            v, a, b, d = spread(Z[n - 1], p, s, m)
            at = pl.ds(s, m)
            Z[n][p, at, :] = v + d * (M[at, :] * scale)
            a, b = ends_off(a, b)
            S[n - 1][p, at, :] = v + (a + b)

    def finish(p, slot):
        for i, z in enumerate((Z1, S2, S3)):
            for s, m in chunks(own0 - 1, rows + 2):
                at = pl.ds(s, m)
                T[slot, i, at, :] = z[p - 1, at, :] + z[p, at, :] + z[p + 1, at, :]
        for s, m in chunks(own0, rows):
            at, lo, hi = pl.ds(s, m), pl.ds(s - 1, m), pl.ds(s + 1, m)
            e1, e2, e3 = V2[p, at, :], V3[p, at, :], spread(V3, p, s, m)[3]
            z1, _, _, d = spread(Z1, p, s, m)
            r1 = e1 + e2
            r2 = r1 + (e2 + e3)
            sums = [T[slot, i, lo, :] + T[slot, i, at, :] + T[slot, i, hi, :] for i in range(3)]
            a, b = ends_off(*turned(sums[0]))
            q1 = sums[0] + (a + b)
            third = 1.0 / 27.0
            total = (e1 * (q1 * third - z1) + r1 * (sums[1] * third - Z2[p, at, :])
                     + r2 * (sums[2] * third - Z[0][p, at, :]))
            out = pl.ds(s - own0, m)
            ind_out[p - HALO, out, :] = total * (-1.0 / (step_size * step_size))
            sens_out[p - HALO, out, :] = (z1 + d) * (1.0 / step_size)

    def each(lo, count, body, unroll=2):
        @pl.loop(0, count // unroll)
        def _(i):
            for j in range(unroll):
                body(lo + i * unroll + j, j)

    pl.semaphore_wait(barrier, sum(there.astype(jnp.int32) for there, _ in sides) - beside.astype(jnp.int32))

    @pl.when(is_first)
    def _():
        for who in (right, up):
            pl.semaphore_signal(late, inc=1, device_id=who, device_id_type=MESH)

    @pl.loop(0, 2)
    def _(side):
        @pl.when(unless(y_to(side), both(beside_y, side == 1)))
        def _():
            start_all(y_copies(side))

        @pl.when(unless(x_to(side), both(beside_x, side == 1)))
        def _():
            x_start(side)

    for load in loads:
        load.wait()
    table = [cond[i] * (0.5 * step_size) for i in range(cond.shape[0])]
    row = lax.broadcasted_iota(jnp.int32, (ext, lanes), 0)
    M[pl.ds(R0, ext), :] = jnp.where(
        both(either(row >= HALO, has_down), either(row < HALO + rows, has_up)), 1.0, 0.0).astype(jnp.float32)
    edge_tiles = (R0, own0 + rows - HALO)

    @pl.loop(0, 3)
    def _(turn):
        own = turn == 0
        high = jnp.where(turn == 1, 1 - odd, odd)
        there = either(own, x_from(high))

        def begin(low_own, low, step):
            return jnp.where(own, low_own, low + step * high)

        def plane_scale(p):
            inside = either(there, both(p >= HALO, p < HALO + depth))
            return jnp.where(inside, 1.0, 0.0).astype(jnp.float32)

        @pl.when(both(there, turn > 0))
        def _():
            @pl.when(unless(turn > 0, both(across, high == 0)))
            def _():
                x_arrive(high)

            other_way = both(beside_x, high == 0)

            @pl.when(other_way)
            def _():
                for copy in e_copies():
                    copy.wait_recv()
                for got, ref in zip((eu, em, eg), edges_of):
                    for j in range(HALO):
                        ref[1, j] = got[j, pl.ds(0, HALO), :]

            @pl.loop(0, 2)
            def _(y_side):
                @pl.when(unless(y_from(y_side), both(other_way, y_side == 1)))
                def _():
                    for copy in c_copies(high, y_side):
                        copy.wait_recv()

        fill_lo = begin(HALO, 0, depth + HALO)
        fill_n = jnp.where(own, depth, HALO)

        @pl.loop(0, fill_n)
        def _(j):
            fill_own(fill_lo + j, there)

        def edges_in():
            @pl.loop(0, fill_n)
            def _(j):
                fill_edges(fill_lo + j, there)

        x_lo, x_n = begin(HALO, 0, depth + HALO - 1), jnp.where(own, depth - 1, HALO)
        lo, step = begin(HALO + 1, 1, depth + 2), jnp.where(own, 1, 1 - 2 * high)

        def count(n):
            return jnp.where(own, depth - 2 - 2 * n, HALO)

        pl.when(turn > 0)(edges_in)

        @pl.loop(0, x_n)
        def _(j):
            faces_x(x_lo + j, R0, ext)

        each(lo, count(0), lambda p, j: faces(p, R0, ext, plane_scale(p)))
        each(lo, count(0), lambda p, j: forward(0, p, R0 + 1, ext - 2, plane_scale(p)))

        for n in (1, 2):
            def both_ways(p, j):
                forward(n, p, R0 + 1, ext - 2, plane_scale(p))
                backward(n, p, R0 + 1, ext - 2, plane_scale(p))
            each(lo + n * step, count(n), both_ways)

        @pl.when(own)
        def _():
            @pl.when(beside_y)
            def _():
                pl.semaphore_wait(late, 1)
                start_all(y_copies(1))

            @pl.when(across)
            def _():
                x_arrive(0)
                start_all(e_copies())

            @pl.when(beside_x)
            def _():
                pl.semaphore_wait(late, 1)
                x_start(1)

            @pl.loop(0, 2)
            def _(y_side):
                @pl.when(y_from(y_side))
                def _():
                    for copy in y_copies(y_side):
                        copy.wait_recv()

                    @pl.loop(0, 2)
                    def _(side):
                        @pl.when(c_sent(side, y_side))
                        def _():
                            start_all(c_copies(side, y_side))

            edges_in()

            @pl.loop(0, x_n)
            def _(j):
                for r in edge_tiles:
                    faces_x(x_lo + j, r, 2 * HALO)

            def edge_faces(p, j):
                for r in edge_tiles:
                    faces(p, r, 2 * HALO, 1.0)
            each(lo, count(0), edge_faces)

            def edge_forward(p, j):
                for r in edge_tiles:
                    forward(0, p, r, 2 * HALO, 1.0)
            each(lo, count(0), edge_forward)

            for n in (1, 2):
                def edge_both(p, j):
                    for r in edge_tiles:
                        forward(n, p, r, 2 * HALO, 1.0)
                        backward(n, p, r, 2 * HALO, 1.0)
                each(lo + n, count(n), edge_both)

        each(begin(2 * HALO, HALO, depth - HALO), jnp.where(own, depth - 2 * HALO, HALO), finish, FINISH)

    @pl.loop(0, 2)
    def _(side):
        @pl.when(y_to(side))
        def _():
            for copy in y_copies(side):
                copy.wait_send()

        @pl.when(x_to(side))
        def _():
            for copy in x_copies(side):
                copy.wait_send()

            @pl.when(side == 0)
            def _():
                x_last(side).wait_send()

        @pl.loop(0, 2)
        def _(y_side):
            @pl.when(c_sent(side, y_side))
            def _():
                for copy in c_copies(side, y_side):
                    copy.wait_send()

    @pl.when(across)
    def _():
        for copy in e_copies():
            copy.wait_send()


def put_out(a, b, a_out, b_out, sem):
    part = a.shape[0] // 4
    copies = [
        pltpu.make_async_copy(src.at[pl.ds(q * part, part)], dst.at[pl.ds(q * part, part)], sem.at[i, q])
        for i, (src, dst) in enumerate(((a, a_out), (b, b_out))) for q in range(4)
    ]
    for copy in copies:
        copy.start()
    for copy in copies:
        copy.wait()


def solution(mesh):
    nx, ny = mesh.shape["gx"], mesh.shape["gy"]

    def step(initial, material, goal_faces, conductivity):
        depth, rows, lanes = initial.shape
        planes, tall = depth + 2 * HALO, rows + 2 * HALO + 16
        f32, i32 = jnp.float32, jnp.int32
        by_rows = (depth, rows // HALO, HALO, lanes)
        halos = []
        for shape in ((planes, rows, lanes), (2, planes, HALO, lanes), (HALO, 2 * HALO, lanes)):
            halos += [pltpu.VMEM(shape, t) for t in (f32, i32, i32)]
        sem = pltpu.SemaphoreType.DMA
        whole = pl.BlockSpec(memory_space=pltpu.MemorySpace.HBM)
        inside = pl.BlockSpec(memory_space=pltpu.VMEM)

        def keep(v):
            return pltpu.with_memory_space_constraint(v, pltpu.MemorySpace.HBM)

        args = (conductivity, initial, material, goal_faces,
                initial.reshape(by_rows), material.reshape(by_rows), goal_faces.reshape(by_rows))
        ind, sens = pl.pallas_call(
            functools.partial(kernel, nx, ny),
            out_shape=[pltpu.VMEM(initial.shape, f32)] * 2,
            in_specs=[whole] * 7,
            out_specs=[inside, inside],
            scratch_shapes=halos
            + [pltpu.VMEM((planes, tall, lanes), f32) for _ in range(16)]
            + [pltpu.VMEM((tall, lanes), f32), pltpu.VMEM((FINISH, 3, tall, lanes), f32)]
            + [pltpu.SMEM(conductivity.shape, f32), sem((4,)), sem((2, 4)), sem((2, 4)),
               sem((2, 3)), sem((2, 3)), sem((2, 2, 3)), sem((2, 2, 3)), sem((3,)), sem((3,)),
               pltpu.SemaphoreType.REGULAR],
            compiler_params=pltpu.CompilerParams(
                collective_id=0, has_side_effects=True, vmem_limit_bytes=50 << 20),
            name="cells",
        )(*(keep(v) for v in args))
        return pl.pallas_call(
            put_out,
            out_shape=[jax.ShapeDtypeStruct(initial.shape, f32)] * 2,
            in_specs=[inside] * 2,
            out_specs=[pl.BlockSpec(memory_space=pl.ANY)] * 2,
            scratch_shapes=[sem((2, 4))],
            compiler_params=pltpu.CompilerParams(vmem_limit_bytes=4 << 20),
            name="put_out",
        )(ind, sens)

    placed = P("gx", "gy", None)
    return jax.shard_map(
        step,
        mesh=mesh,
        in_specs=(placed, placed, placed, P()),
        out_specs=(placed, placed),
        check_vma=False,
    )
```

time: 21 us -> 18.4 us (0.88)
  the two profiles are of different devices: /device:TPU:1 before, /device:TPU:248 now
where the time goes in v4:
time: 18.4 us; the launch traced here: 18.2 us
  Pallas kernels  17.6 us (96%)
  between operations  0.64 us (3%)
    pallas_call x1, Pallas kernels, step(): pl.pallas_call(functools.partial(kernel, nx, ny), out_shape=[pltpu.VMEM(i...  16.6 us
    pallas_call x1, Pallas kernels, step(): pl.pallas_call(put_out, out_shape=[jax.ShapeDtypeStruct(initial.shape, f3...  1.03 us

profile of v4, /device:TPU:248, one launch (start us, length us, event | category | flops | bytes accessed | tf_op | source)
XLA Modules:
  0.0 18.2 jit_solution(18101378991064804202)
XLA Ops:
  0.6 16.6 %cells.1 = (f32[16,64,128]{2,1,0:T(8,128)S(1)}, f32[16,64,128]{2,1,0:T(8,128)S(1)}) custom-call(f32[8]{0:T(128)} %cond_in.1, f32[16,64,128]{2,1,0:T(8,128)} %u_in.1, s32[16,64,128]{2,1,0:T(8,128)} %m_in.1, s32[16,64,128]{2,1,0:T(8,128)} %g_in.1, f32[16,16,4,128]{3,2,1,0:T(4,128)} %bitcast.3, s32[16,16,4,128]{3,2,1,0:T(4,128)} %bitcast.4, ...), custom_call_target="tpu_custom_call" | custom-call | tf_op jit(solution)/shard_map/cells/pallas_call | solution.py:463
  17.2 1.0 %put_out.1 = (f32[16,64,128]{2,1,0:T(8,128)}, f32[16,64,128]{2,1,0:T(8,128)}) custom-call(f32[16,64,128]{2,1,0:T(8,128)S(1)} %get-tuple-element.4.a, f32[16,64,128]{2,1,0:T(8,128)S(1)} %get-tuple-element.5.b), custom_call_target="tpu_custom_call" | custom-call | tf_op jit(solution)/shard_map/put_out/pallas_call | solution.py:478

commit v5 on v4

--- a/solution.py
+++ b/solution.py
@@ -178,22 +178,18 @@
         for side, r in ((0, R0), (1, own0 + rows)):
             fill(p, r, HALO, both(there, y_from(side)), lambda i, m: tuple(ref[side, p] for ref in edges_of))
 
-    def faces_x(p, r, n):
-        for s, m in chunks(r, n):
-            at = pl.ds(s, m)
-            WX[p, at, :] = K[p, at, :] + K[p + 1, at, :]
-
     def faces(p, r, n, scale):
         for s, m in chunks(r, n):
             at, lo, hi = pl.ds(s, m), pl.ds(s - 1, m), pl.ds(s + 1, m)
-            k = K[p, at, :]
+            k, behind = K[p, at, :], K[p - 1, at, :]
             a, b = ends_off(*turned(k))
             h = K[p, hi, :]
             k2 = k + k
             WY[p, at, :] = k + h
             WZ[p, at, :] = jnp.where(lane_is(lanes - 1, m), 0.0, k + a)
             WB[p, at, :] = jnp.where(lane_is(0, m), 0.0, k + b)
-            wx, wx_low = WX[p, at, :], WX[p - 1, at, :]
+            wx, wx_low = k + K[p + 1, at, :], behind + k
+            WX[p, at, :], WX[p - 1, at, :] = wx, wx_low
             C[p, at, :] = ((wx + wx_low) + (k2 + (K[p, lo, :] + h))) + (k2 + (a + b))
             Z[0][p, at, :] = (G[p, at, :] * wx - G[p - 1, at, :] * wx_low) * (M[at, :] * scale)
 
@@ -272,93 +268,90 @@
     row = lax.broadcasted_iota(jnp.int32, (ext, lanes), 0)
     M[pl.ds(R0, ext), :] = jnp.where(
         both(either(row >= HALO, has_down), either(row < HALO + rows, has_up)), 1.0, 0.0).astype(jnp.float32)
-    edge_tiles = (R0, own0 + rows - HALO)
-
-    @pl.loop(0, 3)
+
+    near = 1 - odd
+
+    def corners_in(high):
+        other_way = both(beside_x, high == 0)
+
+        @pl.when(other_way)
+        def _():
+            for copy in e_copies():
+                copy.wait_recv()
+            for got, ref in zip((eu, em, eg), edges_of):
+                for j in range(HALO):
+                    ref[1, j] = got[j, pl.ds(0, HALO), :]
+
+        @pl.loop(0, 2)
+        def _(y_side):
+            @pl.when(unless(y_from(y_side), both(other_way, y_side == 1)))
+            def _():
+                for copy in c_copies(high, y_side):
+                    copy.wait_recv()
+
+    def pair(p, j, tiles, scales):
+        if j == 0:
+            for q, scale in enumerate(scales):
+                for r, n in tiles:
+                    faces(p + q, r, n, scale)
+            for q, scale in enumerate(scales):
+                for r, n in tiles:
+                    forward(0, p + q, max(r, R0 + 1), min(n, ext - 2), scale)
+
+    @pl.loop(0, 3 + beside_x.astype(jnp.int32))
     def _(turn):
-        own = turn == 0
-        high = jnp.where(turn == 1, 1 - odd, odd)
+        own, last = turn == 0, turn >= 2
+        high = jnp.where(unless(last, both(beside_x, turn == 2)), odd, near)
+        idle = both(beside_x, turn == 1)
         there = either(own, x_from(high))
-
-        def begin(low_own, low, step):
-            return jnp.where(own, low_own, low + step * high)
 
         def plane_scale(p):
             inside = either(there, both(p >= HALO, p < HALO + depth))
             return jnp.where(inside, 1.0, 0.0).astype(jnp.float32)
 
-        @pl.when(both(there, turn > 0))
-        def _():
-            @pl.when(unless(turn > 0, both(across, high == 0)))
-            def _():
-                x_arrive(high)
-
-            other_way = both(beside_x, high == 0)
-
-            @pl.when(other_way)
-            def _():
-                for copy in e_copies():
-                    copy.wait_recv()
-                for got, ref in zip((eu, em, eg), edges_of):
-                    for j in range(HALO):
-                        ref[1, j] = got[j, pl.ds(0, HALO), :]
-
-            @pl.loop(0, 2)
-            def _(y_side):
-                @pl.when(unless(y_from(y_side), both(other_way, y_side == 1)))
-                def _():
-                    for copy in c_copies(high, y_side):
-                        copy.wait_recv()
-
-        fill_lo = begin(HALO, 0, depth + HALO)
-        fill_n = jnp.where(own, depth, HALO)
-
-        @pl.loop(0, fill_n)
+        @pl.when(both(there, unless(turn > 0, idle)))
+        def _():
+            x_arrive(high)
+
+            @pl.when(both(across, turn == 1))
+            def _():
+                start_all(e_copies())
+
+            @pl.when(last)
+            def _():
+                corners_in(high)
+
+        def span(own):
+            fill_lo = jnp.where(own, HALO, (depth + HALO) * high)
+            lo, step = jnp.where(own, HALO + 1, 1 + (depth + 2) * high), jnp.where(own, 1, 1 - 2 * high)
+            return fill_lo, jnp.where(own, depth, HALO), lo, step
+
+        def count(own, n):
+            return jnp.where(own, depth - 2 - 2 * n, HALO)
+
+        fill_lo, fill_n, lo, step = span(own)
+
+        @pl.loop(0, jnp.where(idle, 0, fill_n))
         def _(j):
             fill_own(fill_lo + j, there)
 
-        def edges_in():
-            @pl.loop(0, fill_n)
-            def _(j):
-                fill_edges(fill_lo + j, there)
-
-        x_lo, x_n = begin(HALO, 0, depth + HALO - 1), jnp.where(own, depth - 1, HALO)
-        lo, step = begin(HALO + 1, 1, depth + 2), jnp.where(own, 1, 1 - 2 * high)
-
-        def count(n):
-            return jnp.where(own, depth - 2 - 2 * n, HALO)
-
-        pl.when(turn > 0)(edges_in)
-
-        @pl.loop(0, x_n)
-        def _(j):
-            faces_x(x_lo + j, R0, ext)
-
-        each(lo, count(0), lambda p, j: faces(p, R0, ext, plane_scale(p)))
-        each(lo, count(0), lambda p, j: forward(0, p, R0 + 1, ext - 2, plane_scale(p)))
-
+        @pl.when(last)
+        def _():
+            each(fill_lo, HALO, lambda p, j: fill_edges(p, there), HALO)
+
+        each(lo, jnp.where(idle, 0, count(own, 0)), lambda p, j: pair(p, j, ((R0, ext),), (plane_scale(p), plane_scale(p + 1))))
         for n in (1, 2):
             def both_ways(p, j):
                 forward(n, p, R0 + 1, ext - 2, plane_scale(p))
                 backward(n, p, R0 + 1, ext - 2, plane_scale(p))
-            each(lo + n * step, count(n), both_ways)
-
-        @pl.when(own)
+            each(lo + n * step, jnp.where(idle, 0, count(own, n)), both_ways)
+
+        @pl.when(turn == 1)
         def _():
             @pl.when(beside_y)
             def _():
                 pl.semaphore_wait(late, 1)
                 start_all(y_copies(1))
-
-            @pl.when(across)
-            def _():
-                x_arrive(0)
-                start_all(e_copies())
-
-            @pl.when(beside_x)
-            def _():
-                pl.semaphore_wait(late, 1)
-                x_start(1)
 
             @pl.loop(0, 2)
             def _(y_side):
@@ -369,35 +362,35 @@
 
                     @pl.loop(0, 2)
                     def _(side):
-                        @pl.when(c_sent(side, y_side))
+                        @pl.when(unless(c_sent(side, y_side), both(beside_x, side == 1)))
                         def _():
                             start_all(c_copies(side, y_side))
 
-            edges_in()
-
-            @pl.loop(0, x_n)
-            def _(j):
-                for r in edge_tiles:
-                    faces_x(x_lo + j, r, 2 * HALO)
-
-            def edge_faces(p, j):
-                for r in edge_tiles:
-                    faces(p, r, 2 * HALO, 1.0)
-            each(lo, count(0), edge_faces)
-
-            def edge_forward(p, j):
-                for r in edge_tiles:
-                    forward(0, p, r, 2 * HALO, 1.0)
-            each(lo, count(0), edge_forward)
-
-            for n in (1, 2):
-                def edge_both(p, j):
-                    for r in edge_tiles:
-                        forward(n, p, r, 2 * HALO, 1.0)
-                        backward(n, p, r, 2 * HALO, 1.0)
-                each(lo + n, count(n), edge_both)
-
-        each(begin(2 * HALO, HALO, depth - HALO), jnp.where(own, depth - 2 * HALO, HALO), finish, FINISH)
+            tiles = ((R0, 2 * HALO), (own0 + rows - HALO, 2 * HALO))
+
+            @pl.loop(0, jnp.where(idle, 1, 2))
+            def _(part):
+                mine = part == 0
+                pl.when(part == 1)(lambda: corners_in(near))
+                fill_lo, fill_n, lo, step = span(mine)
+                each(fill_lo, fill_n, lambda p, j: fill_edges(p, True), HALO)
+                each(lo, count(mine, 0), lambda p, j: pair(p, j, tiles, (1.0, 1.0)))
+                for n in (1, 2):
+                    def edge_both(p, j):
+                        for r, m in tiles:
+                            forward(n, p, r, m, 1.0)
+                            backward(n, p, r, m, 1.0)
+                    each(lo + n * step, count(mine, n), edge_both)
+
+            @pl.when(beside_x)
+            def _():
+                pl.semaphore_wait(late, 1)
+                x_start(1)
+                start_all(c_copies(1, 1))
+
+        done_lo = jnp.where(last, HALO + high * (depth - HALO), jnp.where(idle, 2 * HALO, HALO + high * HALO))
+        done_n = jnp.where(last, HALO, jnp.where(idle, depth - 2 * HALO, depth - HALO))
+        each(done_lo, jnp.where(own, 0, done_n), finish, FINISH)
 
     @pl.loop(0, 2)
     def _(side):

time: 18.4 us -> 16.8 us (0.913)
  Pallas kernels: 17.6 us -> 16 us
    pallas_call x1, Pallas kernels: 16.6 us -> 15 us  [step(): pl.pallas_call(functools.partial(kernel, nx, ny), out_shape=[pltpu.VMEM(i...]
where the time goes in v5:
time: 16.8 us; the launch traced here: 16.6 us
  Pallas kernels  16 us (95%)
  between operations  0.64 us (4%)
    pallas_call x1, Pallas kernels, step(): pl.pallas_call(functools.partial(kernel, nx, ny), out_shape=[pltpu.VMEM(i...  15 us
    pallas_call x1, Pallas kernels, step(): pl.pallas_call(put_out, out_shape=[jax.ShapeDtypeStruct(initial.shape, f3...  1.03 us

profile of v5, /device:TPU:248, one launch (start us, length us, event | category | flops | bytes accessed | tf_op | source)
XLA Modules:
  0.0 16.6 jit_solution(6962238128811830006)
XLA Ops:
  0.6 15.0 %cells.1 = (f32[16,64,128]{2,1,0:T(8,128)S(1)}, f32[16,64,128]{2,1,0:T(8,128)S(1)}) custom-call(f32[8]{0:T(128)} %cond_in.1, f32[16,64,128]{2,1,0:T(8,128)} %u_in.1, s32[16,64,128]{2,1,0:T(8,128)} %m_in.1, s32[16,64,128]{2,1,0:T(8,128)} %g_in.1, f32[16,16,4,128]{3,2,1,0:T(4,128)} %bitcast.3, s32[16,16,4,128]{3,2,1,0:T(4,128)} %bitcast.4, ...), custom_call_target="tpu_custom_call" | custom-call | tf_op jit(solution)/shard_map/cells/pallas_call | solution.py:456
  15.6 1.0 %put_out.1 = (f32[16,64,128]{2,1,0:T(8,128)}, f32[16,64,128]{2,1,0:T(8,128)}) custom-call(f32[16,64,128]{2,1,0:T(8,128)S(1)} %get-tuple-element.4.a, f32[16,64,128]{2,1,0:T(8,128)S(1)} %get-tuple-element.5.b), custom_call_target="tpu_custom_call" | custom-call | tf_op jit(solution)/shard_map/put_out/pallas_call | solution.py:471

commit v6 on v5

--- a/solution.py
+++ b/solution.py
@@ -13,14 +13,81 @@
 R0 = 8
 CHUNK = 8
 FINISH = 2
+LANES = 128
+
+
+def turned(v):
+    return pltpu.roll(v, LANES - 1, 1), pltpu.roll(v, 1, 1)
+
+
+def lane_is(which, n):
+    return lax.broadcasted_iota(jnp.int32, (n, LANES), 1) == which
+
+
+def ends_off(a, b):
+    n = a.shape[0]
+    return jnp.where(lane_is(LANES - 1, n), 0.0, a), jnp.where(lane_is(0, n), 0.0, b)
+
+
+def chunks(r, n):
+    while n > 0:
+        yield r, min(n, CHUNK)
+        r, n = r + CHUNK, n - CHUNK
+
+
+def each(lo, count, body, unroll=2):
+    @pl.loop(0, count // unroll)
+    def _(i):
+        for j in range(unroll):
+            body(lo + i * unroll + j, j)
+
+
+def spread_with(weights, src, p, s, m):
+    WX, WY, WZ, WB, C = weights
+    at, lo, hi = pl.ds(s, m), pl.ds(s - 1, m), pl.ds(s + 1, m)
+    v = src[p, at, :]
+    a, b = turned(v)
+    d = (
+        (WX[p, at, :] * src[p + 1, at, :] + WX[p - 1, at, :] * src[p - 1, at, :])
+        + (WY[p, at, :] * src[p, hi, :] + WY[p, lo, :] * src[p, lo, :])
+        + (WZ[p, at, :] * a + WB[p, at, :] * b)
+        - C[p, at, :] * v
+    )
+    return v, a, b, d
+
+
+def finish(weights, fields, T, outs, p, slot, tiles):
+    V2, V3, Z3, Z2, Z1, S3, S2 = fields
+    own0 = R0 + HALO
+    for r, n in tiles:
+        for i, z in enumerate((Z1, S2, S3)):
+            for s, m in chunks(r - 1, n + 2):
+                at = pl.ds(s, m)
+                T[slot, i, at, :] = z[p - 1, at, :] + z[p, at, :] + z[p + 1, at, :]
+    for r, n in tiles:
+        for s, m in chunks(r, n):
+            at, lo, hi = pl.ds(s, m), pl.ds(s - 1, m), pl.ds(s + 1, m)
+            e1, e2, e3 = V2[p, at, :], V3[p, at, :], spread_with(weights, V3, p, s, m)[3]
+            z1, _, _, d = spread_with(weights, Z1, p, s, m)
+            r1 = e1 + e2
+            r2 = r1 + (e2 + e3)
+            sums = [T[slot, i, lo, :] + T[slot, i, at, :] + T[slot, i, hi, :] for i in range(3)]
+            a, b = ends_off(*turned(sums[0]))
+            q1 = sums[0] + (a + b)
+            third = 1.0 / 27.0
+            total = (e1 * (q1 * third - z1) + r1 * (sums[1] * third - Z2[p, at, :])
+                     + r2 * (sums[2] * third - Z3[p, at, :])) * (-1.0 / (step_size * step_size))
+            out = pl.ds(s - own0, m)
+            outs[0][p - HALO, out, :] = total
+            outs[1][p - HALO, out, :] = (z1 + d) * (1.0 / step_size)
 
 
 def kernel(
     nx, ny, cond_in,
     u_in, m_in, g_in, u_rows, m_rows, g_rows,
-    ind_out, sens_out,
+    ind_out, sens_out, WX, WY, WZ, WB, C, V2, V3, Z3, Z2, Z1, S3, S2,
     u_all, m_all, g_all, u_edge, m_edge, g_edge, eu, em, eg,
-    K, WX, WY, WZ, WB, C, G, V0, V1, V2, V3, Z3, Z2, Z1, S3, S2, M, T,
+    K, G, V0, V1, M, T,
     cond, load_sem, x_send, x_recv, y_send, y_recv, c_send, c_recv, e_send, e_recv, late,
 ):
     depth, rows, lanes = u_in.shape
@@ -144,21 +211,6 @@
         def _():
             x_last(side).wait_recv()
 
-    def turned(v):
-        return pltpu.roll(v, lanes - 1, 1), pltpu.roll(v, 1, 1)
-
-    def lane_is(which, n):
-        return lax.broadcasted_iota(jnp.int32, (n, lanes), 1) == which
-
-    def ends_off(a, b):
-        n = a.shape[0]
-        return jnp.where(lane_is(lanes - 1, n), 0.0, a), jnp.where(lane_is(0, n), 0.0, b)
-
-    def chunks(r, n):
-        while n > 0:
-            yield r, min(n, CHUNK)
-            r, n = r + CHUNK, n - CHUNK
-
     def fill(p, r, n, there, read):
         for i in range(0, n, CHUNK):
             m = min(CHUNK, n - i)
@@ -177,6 +229,11 @@
     def fill_edges(p, there):
         for side, r in ((0, R0), (1, own0 + rows)):
             fill(p, r, HALO, both(there, y_from(side)), lambda i, m: tuple(ref[side, p] for ref in edges_of))
+
+    def kept(s, m, scale):
+        if own0 <= s and s + m <= own0 + rows:
+            return scale
+        return M[pl.ds(s, m), :] * scale
 
     def faces(p, r, n, scale):
         for s, m in chunks(r, n):
@@ -191,59 +248,26 @@
             wx, wx_low = k + K[p + 1, at, :], behind + k
             WX[p, at, :], WX[p - 1, at, :] = wx, wx_low
             C[p, at, :] = ((wx + wx_low) + (k2 + (K[p, lo, :] + h))) + (k2 + (a + b))
-            Z[0][p, at, :] = (G[p, at, :] * wx - G[p - 1, at, :] * wx_low) * (M[at, :] * scale)
+            Z[0][p, at, :] = (G[p, at, :] * wx - G[p - 1, at, :] * wx_low) * kept(s, m, scale)
+
+    weights = (WX, WY, WZ, WB, C)
+    fields = (V2, V3, Z3, Z2, Z1, S3, S2)
 
     def spread(src, p, s, m):
-        at, lo, hi = pl.ds(s, m), pl.ds(s - 1, m), pl.ds(s + 1, m)
-        v = src[p, at, :]
-        a, b = turned(v)
-        d = (
-            (WX[p, at, :] * src[p + 1, at, :] + WX[p - 1, at, :] * src[p - 1, at, :])
-            + (WY[p, at, :] * src[p, hi, :] + WY[p, lo, :] * src[p, lo, :])
-            + (WZ[p, at, :] * a + WB[p, at, :] * b)
-            - C[p, at, :] * v
-        )
-        return v, a, b, d
+        return spread_with(weights, src, p, s, m)
 
     def forward(n, p, r, k, scale):
         for s, m in chunks(r, k):
             at = pl.ds(s, m)
-            V[n + 1][p, at, :] = spread(V[n], p, s, m)[3] * (M[at, :] * scale)
+            V[n + 1][p, at, :] = spread(V[n], p, s, m)[3] * kept(s, m, scale)
 
     def backward(n, p, r, k, scale):
         for s, m in chunks(r, k):
             v, a, b, d = spread(Z[n - 1], p, s, m)
             at = pl.ds(s, m)
-            Z[n][p, at, :] = v + d * (M[at, :] * scale)
+            Z[n][p, at, :] = v + d * kept(s, m, scale)
             a, b = ends_off(a, b)
             S[n - 1][p, at, :] = v + (a + b)
-
-    def finish(p, slot):
-        for i, z in enumerate((Z1, S2, S3)):
-            for s, m in chunks(own0 - 1, rows + 2):
-                at = pl.ds(s, m)
-                T[slot, i, at, :] = z[p - 1, at, :] + z[p, at, :] + z[p + 1, at, :]
-        for s, m in chunks(own0, rows):
-            at, lo, hi = pl.ds(s, m), pl.ds(s - 1, m), pl.ds(s + 1, m)
-            e1, e2, e3 = V2[p, at, :], V3[p, at, :], spread(V3, p, s, m)[3]
-            z1, _, _, d = spread(Z1, p, s, m)
-            r1 = e1 + e2
-            r2 = r1 + (e2 + e3)
-            sums = [T[slot, i, lo, :] + T[slot, i, at, :] + T[slot, i, hi, :] for i in range(3)]
-            a, b = ends_off(*turned(sums[0]))
-            q1 = sums[0] + (a + b)
-            third = 1.0 / 27.0
-            total = (e1 * (q1 * third - z1) + r1 * (sums[1] * third - Z2[p, at, :])
-                     + r2 * (sums[2] * third - Z[0][p, at, :]))
-            out = pl.ds(s - own0, m)
-            ind_out[p - HALO, out, :] = total * (-1.0 / (step_size * step_size))
-            sens_out[p - HALO, out, :] = (z1 + d) * (1.0 / step_size)
-
-    def each(lo, count, body, unroll=2):
-        @pl.loop(0, count // unroll)
-        def _(i):
-            for j in range(unroll):
-                body(lo + i * unroll + j, j)
 
     pl.semaphore_wait(barrier, sum(there.astype(jnp.int32) for there, _ in sides) - beside.astype(jnp.int32))
 
@@ -388,9 +412,11 @@
                 x_start(1)
                 start_all(c_copies(1, 1))
 
+        late_turn = both(beside_x, turn == 2)
         done_lo = jnp.where(last, HALO + high * (depth - HALO), jnp.where(idle, 2 * HALO, HALO + high * HALO))
-        done_n = jnp.where(last, HALO, jnp.where(idle, depth - 2 * HALO, depth - HALO))
-        each(done_lo, jnp.where(own, 0, done_n), finish, FINISH)
+        done_n = jnp.where(turn == 1, jnp.where(idle, depth - 2 * HALO, depth - HALO), jnp.where(late_turn, HALO, 0))
+        each(done_lo, done_n, lambda p, j: finish(
+            weights, fields, T, (ind_out, sens_out), p, j, ((own0, rows),)), FINISH)
 
     @pl.loop(0, 2)
     def _(side):
@@ -421,15 +447,26 @@
             copy.wait_send()
 
 
-def put_out(a, b, a_out, b_out, sem):
-    part = a.shape[0] // 4
+def put_out(*refs):
+    done, refs = refs[:2], refs[2:]
+    weights, fields, outs, last, T, sem = refs[:5], refs[5:12], refs[12:14], refs[14:16], refs[16], refs[17]
+    depth, rows, _ = done[0].shape
+    odd = lax.rem(lax.axis_index("gx"), 2)
+    first, part = HALO * (1 - odd), (depth - HALO) // 3
     copies = [
-        pltpu.make_async_copy(src.at[pl.ds(q * part, part)], dst.at[pl.ds(q * part, part)], sem.at[i, q])
-        for i, (src, dst) in enumerate(((a, a_out), (b, b_out))) for q in range(4)
+        pltpu.make_async_copy(done[i].at[at], outs[i].at[at], sem.at[i, q])
+        for q in range(3) for i in range(2) for at in (pl.ds(first + q * part, part),)
     ]
     for copy in copies:
         copy.start()
-    for copy in copies:
+    begin = HALO + odd * (depth - HALO)
+    own0 = R0 + HALO
+    each(begin, HALO, lambda p, j: finish(weights, fields, T, last, p, j, ((own0, rows),)), FINISH)
+    at = pl.ds(odd * (depth - HALO), HALO)
+    rest = [pltpu.make_async_copy(last[i].at[at], outs[i].at[at], sem.at[i, 3]) for i in range(2)]
+    for copy in rest:
+        copy.start()
+    for copy in copies + rest:
         copy.wait()
 
 
@@ -453,30 +490,32 @@
 
         args = (conductivity, initial, material, goal_faces,
                 initial.reshape(by_rows), material.reshape(by_rows), goal_faces.reshape(by_rows))
-        ind, sens = pl.pallas_call(
+        field = pltpu.VMEM((planes, tall, lanes), f32)
+        block = pltpu.VMEM(initial.shape, f32)
+        made = pl.pallas_call(
             functools.partial(kernel, nx, ny),
-            out_shape=[pltpu.VMEM(initial.shape, f32)] * 2,
+            out_shape=[block] * 2 + [field] * 12,
             in_specs=[whole] * 7,
-            out_specs=[inside, inside],
+            out_specs=[inside] * 14,
             scratch_shapes=halos
-            + [pltpu.VMEM((planes, tall, lanes), f32) for _ in range(16)]
+            + [field] * 4
             + [pltpu.VMEM((tall, lanes), f32), pltpu.VMEM((FINISH, 3, tall, lanes), f32)]
             + [pltpu.SMEM(conductivity.shape, f32), sem((4,)), sem((2, 4)), sem((2, 4)),
                sem((2, 3)), sem((2, 3)), sem((2, 2, 3)), sem((2, 2, 3)), sem((3,)), sem((3,)),
                pltpu.SemaphoreType.REGULAR],
             compiler_params=pltpu.CompilerParams(
-                collective_id=0, has_side_effects=True, vmem_limit_bytes=50 << 20),
+                collective_id=0, has_side_effects=True, vmem_limit_bytes=30 << 20),
             name="cells",
         )(*(keep(v) for v in args))
         return pl.pallas_call(
             put_out,
             out_shape=[jax.ShapeDtypeStruct(initial.shape, f32)] * 2,
-            in_specs=[inside] * 2,
+            in_specs=[inside] * 14,
             out_specs=[pl.BlockSpec(memory_space=pl.ANY)] * 2,
-            scratch_shapes=[sem((2, 4))],
-            compiler_params=pltpu.CompilerParams(vmem_limit_bytes=4 << 20),
+            scratch_shapes=[block] * 2 + [pltpu.VMEM((FINISH, 3, tall, lanes), f32), sem((2, 4))],
+            compiler_params=pltpu.CompilerParams(vmem_limit_bytes=8 << 20),
             name="put_out",
-        )(ind, sens)
+        )(*made)
 
     placed = P("gx", "gy", None)
     return jax.shard_map(

time: 16.8 us -> 16.6 us (0.988)
  Pallas kernels: 16 us -> 15.8 us
    pallas_call x1, Pallas kernels: 15 us -> 14.6 us  [step(): pl.pallas_call(functools.partial(kernel, nx, ny), out_shape=[block] * 2 +...]
    pallas_call x1, Pallas kernels: 1.03 us -> 1.21 us  [step(): pl.pallas_call(put_out, out_shape=[jax.ShapeDtypeStruct(initial.shape, f3...]
where the time goes in v6:
time: 16.6 us; the launch traced here: 16.4 us
  Pallas kernels  15.8 us (95%)
  between operations  0.64 us (4%)
    pallas_call x1, Pallas kernels, step(): pl.pallas_call(functools.partial(kernel, nx, ny), out_shape=[block] * 2 +...  14.6 us
    pallas_call x1, Pallas kernels, step(): pl.pallas_call(put_out, out_shape=[jax.ShapeDtypeStruct(initial.shape, f3...  1.21 us

profile of v6, /device:TPU:248, one launch (start us, length us, event | category | flops | bytes accessed | tf_op | source)
XLA Modules:
  0.0 16.4 jit_solution(2732957779050148929)
XLA Ops:
  0.6 14.6 %cells.1 = (f32[16,64,128]{2,1,0:T(8,128)S(1)}, f32[16,64,128]{2,1,0:T(8,128)S(1)}, f32[24,88,128]{2,1,0:T(8,128)S(1)}, f32[24,88,128]{2,1,0:T(8,128)S(1)}, f32[...) custom-call(f32[8]{0:T(128)} %cond_in.1, ...), custom_call_target="tpu_custom_call" | custom-call | tf_op jit(solution)/shard_map/cells/pallas_call | solution.py:495
  15.2 1.2 %put_out.1 = (f32[16,64,128]{2,1,0:T(8,128)}, f32[16,64,128]{2,1,0:T(8,128)}) custom-call(f32[16,64,128]{2,1,0:T(8,128)S(1)} %get-tuple-element.16.refs_0_, f32[16,64,128]{2,1,0:T(8,128)S(1)} %get-tuple-element.17.refs_1_, f32[24,88,128]{2,1,0:T(8,128)S(1)} %get-tuple-element.18.refs_2_, f32[24,88,128]{2,1,0:T(8,128)S(1)} %get-tuple-element.19.refs_3_, ...), custom_call_target="tpu_custom_call" | custom-call | tf_op jit(solution)/shard_map/put_out/pallas_call | solution.py:510

commit v7 on v6

--- a/solution.py
+++ b/solution.py
@@ -282,6 +282,8 @@
         def _():
             start_all(y_copies(side))
 
+    @pl.loop(0, 2)
+    def _(side):
         @pl.when(unless(x_to(side), both(beside_x, side == 1)))
         def _():
             x_start(side)

time: 16.6 us -> 16.6 us (level)
  no operation moved by 1% of the time
where the time goes in v7:
time: 16.6 us; the launch traced here: 16.4 us
  Pallas kernels  15.8 us (95%)
  between operations  0.64 us (4%)
    pallas_call x1, Pallas kernels, step(): pl.pallas_call(functools.partial(kernel, nx, ny), out_shape=[block] * 2 +...  14.6 us
    pallas_call x1, Pallas kernels, step(): pl.pallas_call(put_out, out_shape=[jax.ShapeDtypeStruct(initial.shape, f3...  1.21 us

profile of v7, /device:TPU:248, one launch (start us, length us, event | category | flops | bytes accessed | tf_op | source)
XLA Modules:
  0.0 16.4 jit_solution(7199584030892395960)
XLA Ops:
  0.6 14.6 %cells.1 = (f32[16,64,128]{2,1,0:T(8,128)S(1)}, f32[16,64,128]{2,1,0:T(8,128)S(1)}, f32[24,88,128]{2,1,0:T(8,128)S(1)}, f32[24,88,128]{2,1,0:T(8,128)S(1)}, f32[...) custom-call(f32[8]{0:T(128)} %cond_in.1, ...), custom_call_target="tpu_custom_call" | custom-call | tf_op jit(solution)/shard_map/cells/pallas_call | solution.py:497
  15.2 1.2 %put_out.1 = (f32[16,64,128]{2,1,0:T(8,128)}, f32[16,64,128]{2,1,0:T(8,128)}) custom-call(f32[16,64,128]{2,1,0:T(8,128)S(1)} %get-tuple-element.16.refs_0_, f32[16,64,128]{2,1,0:T(8,128)S(1)} %get-tuple-element.17.refs_1_, f32[24,88,128]{2,1,0:T(8,128)S(1)} %get-tuple-element.18.refs_2_, f32[24,88,128]{2,1,0:T(8,128)S(1)} %get-tuple-element.19.refs_3_, ...), custom_call_target="tpu_custom_call" | custom-call | tf_op jit(solution)/shard_map/put_out/pallas_call | solution.py:512
